TPU v7x, 32 devices: a whole 2x2x4 slice. The times are simulated.
32 devices in a mesh: parts: 2 (over y), leaf: 4 (over z), vec: 2 (over x), sub: 2 (over core).
Axes of the slice: x: 2, y: 2, z: 4, core: 2. Of those that a mesh axis runs over, the one named last changes fastest.
Arguments:
- charges: float32 [64, 131072], P('vec', ('parts', 'leaf', 'sub')), parts along dimension 1, may hold values from -6 to 6
- coordinates: float32 [3, 131072], P(None, ('parts', 'leaf', 'sub')), parts along dimension 1, may hold values from 0 to 1, as said below
- near_lists: int32 [512, 8], P(('parts', 'leaf', 'sub')), parts along dimension 0, may hold values from -1 to 255, as said below
- far_lists: int32 [1008, 8], P(('parts', 'leaf', 'sub')), parts along dimension 0, may hold values from -1 to 503, as said below
- leaf_basis: float32 [512, 64, 256], P(('parts', 'leaf', 'sub')), parts along dimension 0, may hold values from -0.375 to 0.375
- local_transfer: float32 [496, 64, 128], P(('parts', 'leaf', 'sub')), parts along dimension 0, may hold values from -0.5 to 0.5
- skeleton: float32 [1008, 3, 64], P('parts'), parts along dimension 0, may hold values from 0 to 1
- top_transfer: float32 [12, 64, 128], P('parts'), parts along dimension 0, may hold values from -0.5 to 0.5
- top_skeleton: float32 [12, 3, 64], P('parts'), parts along dimension 0, may hold values from 0 to 1
Outputs:
- potentials: float32 [64, 131072], P('vec', ('parts', 'leaf', 'sub')), parts along dimension 1
There are 2 independent parts, one for each index of `parts`. A program takes and returns all parts, laid end to end along the dimension named above; each array names one. Nothing has to cross between parts.
Inputs may be any that keep to these rules, and one draw needn't show every extreme that they name: `near_lists`: each leaf's list holds the leaf itself in slot 0 and in slot 1 the leaf 16 below it (above it where there is none); every entry lies within 16 leaves of its leaf; empty slots hold -1. `far_lists`: every entry names a cluster of the same level in the same subtree or in one of the two subtrees beside it; slot 0 is always filled and empty slots hold -1. `coordinates`: each leaf's points lie in a box of up to three Morton cells along each dimension that contains the leaf's own Morton cell.
All inputs are finite; a program needn't handle non-finite values.
Results may differ from a plain program's by a relative error of at most 0.0003.
Values sent between devices are 32-bit elements; how exact they have to be, the bound alone decides.
No kernel may reach another device: no remote copies, remote signals or barrier semaphores. Data moves between devices by JAX's collectives and lax.ppermute only.
A program may use at most 64 MiB of HBM per device.

v0:
```python
import jax
import jax.numpy as jnp
from jax import lax
from jax.sharding import PartitionSpec as P

LEAF_PTS = 256
RANK = 64
LEAF_DEV = 32
NODE_DEV = 63
NEAR_REACH = 16


KERNEL_WIDTH = 0.05
NEAR_WEIGHT = 0.0625
exact_mode = lax.Precision.HIGHEST


def with_halo(shard, sides, width):
    for axis, dim in sides:
        size, length = (lax.axis_size(axis), shard.shape[dim])
        up = [(i, (i + 1) % size) for i in range(size - 1)]
        down = [(j, i) for i, j in up]
        last = lax.slice_in_dim(shard, length - width, length, axis=dim)
        first = lax.slice_in_dim(shard, 0, width, axis=dim)
        before = lax.ppermute(last, axis, up)
        after = lax.ppermute(first, axis, down)
        shard = jnp.concatenate([before, shard, after], axis=dim)
    return shard


def swapped(value, axis, stride):
    mask = 2**stride
    pairs = [(source, source ^ mask) for source in range(lax.axis_size(axis))]
    return lax.ppermute(value, axis, pairs)


def kernel_block(targets, sources):
    total = None
    for axis_pos in range(3):
        differ = targets[..., axis_pos, :, None] - sources[..., axis_pos, None, :]
        total = differ * differ if total is None else total + differ * differ
    return KERNEL_WIDTH / jnp.sqrt(total + KERNEL_WIDTH * KERNEL_WIDTH)


def near_field(near_lists, own_points, source_points_all, source_charges_all, first_leaf, extended):

    def near_block(start):
        rows = lax.dynamic_slice_in_dim(near_lists, start, 4, 0)
        valid = (rows >= 0).astype(jnp.float32)
        picked = jnp.clip(rows - first_leaf + NEAR_REACH, 0, extended - 1)
        targets = lax.dynamic_slice_in_dim(own_points, start, 4, 0)
        source_points = source_points_all[picked]
        source_charges = source_charges_all[picked] * valid[:, :, None, None]
        tiles = kernel_block(targets[:, None], source_points)
        return jnp.einsum("betd,bevd->bvt", tiles, source_charges, precision=exact_mode)

    block_starts = jnp.arange(LEAF_DEV // 4) * 4
    result = lax.map(near_block, block_starts)
    return result.reshape(LEAF_DEV, result.shape[2], result.shape[3])


def on_device(
    charges,
    coordinates,
    near_lists,
    far_lists,
    leaf_basis,
    local_transfer,
    skeleton,
    top_transfer,
    top_skeleton,
):
    vectors = charges.shape[0]
    device = lax.axis_index(("leaf", "sub"))
    groups = lax.axis_size(("leaf", "sub"))
    extended = LEAF_DEV + 2 * NEAR_REACH
    own_points = coordinates.reshape(3, LEAF_DEV, LEAF_PTS).transpose(1, 0, 2)
    own_charges = charges.reshape(vectors, LEAF_DEV, LEAF_PTS).transpose(1, 0, 2)
    first_leaf = device * LEAF_DEV
    current = jnp.einsum("kvd,krd->kvr", own_charges, leaf_basis, precision=exact_mode)
    level_coefs = [current]
    level_sizes = [LEAF_DEV]
    level_starts = [0]
    count = LEAF_DEV
    slot_start = 0
    while count > 1:
        half = count // 2
        slot_start = slot_start + count
        paired = (
            current.reshape(half, 2, vectors, RANK)
            .transpose(0, 2, 1, 3)
            .reshape(half, vectors, 2 * RANK)
        )
        mats = local_transfer[slot_start - LEAF_DEV : slot_start - LEAF_DEV + half]
        current = jnp.einsum("hva,hra->hvr", paired, mats, precision=exact_mode)
        level_coefs.append(current)
        level_sizes.append(half)
        level_starts.append(slot_start)
        count = half
    node_coef = jnp.concatenate(level_coefs, axis=0)
    packed = node_coef.transpose(1, 0, 2).reshape(vectors, NODE_DEV * RANK)
    padded_charges, padded_points = (
        with_halo(charges, ((("leaf", "sub"), 1),), NEAR_REACH * LEAF_PTS),
        with_halo(coordinates, ((("leaf", "sub"), 1),), NEAR_REACH * LEAF_PTS),
    )
    padded_coef = with_halo(packed, ((("leaf", "sub"), 1),), NODE_DEV * RANK)
    source_charges_all = padded_charges.reshape(vectors, extended, LEAF_PTS).transpose(1, 0, 2)
    source_points_all = padded_points.reshape(3, extended, LEAF_PTS).transpose(1, 0, 2)
    near = near_field(
        near_lists, own_points, source_points_all, source_charges_all, first_leaf, extended
    )
    base = (device - 1) * NODE_DEV
    span = 3 * NODE_DEV
    source_table = padded_coef.reshape(vectors, span, RANK).transpose(1, 0, 2)
    valid = (far_lists >= 0).astype(jnp.float32)
    global_pick = jnp.clip(far_lists, 0, groups * NODE_DEV - 1)
    local_pick = jnp.clip(far_lists - base, 0, span - 1)
    source_coef = source_table[local_pick] * valid[:, :, None, None]
    source_skel = skeleton[global_pick]
    own_skel = lax.dynamic_slice_in_dim(skeleton, device * NODE_DEV, NODE_DEV, 0)
    tiles = kernel_block(own_skel[:, None], source_skel)
    far = jnp.einsum("nerj,nevj->nvr", tiles, source_coef, precision=exact_mode)
    root = node_coef[NODE_DEV - 1]
    top_bits = groups.bit_length() - 1
    current = root
    couplings = []
    for height in range(top_bits):
        partner = swapped(current, ("leaf", "sub"), height)
        node_id = device // 2**height
        sibling_id = node_id + 1 - 2 * (node_id % 2)
        if height == 0:
            node_skel = own_skel[NODE_DEV - 1]
            partner_skel = skeleton[sibling_id * NODE_DEV + NODE_DEV - 1]
        else:
            start = groups - (groups >> height - 1)
            node_skel = top_skeleton[start + node_id]
            partner_skel = top_skeleton[start + sibling_id]
        pair_tiles = kernel_block(node_skel, partner_skel)
        couplings.append(jnp.dot(partner, pair_tiles.T, precision=exact_mode))
        if height < top_bits - 1:
            upper = node_id % 2 == 1
            lower_part = jnp.where(upper, partner, current)
            upper_part = jnp.where(upper, current, partner)
            paired = jnp.concatenate([lower_part, upper_part], axis=1)
            matrix = top_transfer[groups - (groups >> height) + node_id // 2]
            current = jnp.dot(paired, matrix.T, precision=exact_mode)
    local_root = couplings[top_bits - 1]
    for height in range(top_bits - 2, -1, -1):
        node_id = device // 2**height
        matrix = top_transfer[groups - (groups >> height) + node_id // 2]
        spread = jnp.dot(local_root, matrix, precision=exact_mode)
        mine = jnp.where(node_id % 2 == 1, spread[:, RANK:], spread[:, :RANK])
        local_root = couplings[height] + mine
    level_locals = [
        far[level_starts[pos] : level_starts[pos] + level_sizes[pos]]
        for pos in range(len(level_sizes))
    ]
    level_locals[-1] = level_locals[-1] + local_root[None]
    for pos in range(len(level_sizes) - 2, -1, -1):
        parent = level_locals[pos + 1]
        parent_count = level_sizes[pos + 1]
        first = level_starts[pos + 1] - LEAF_DEV
        mats = local_transfer[first : first + parent_count]
        spread = jnp.einsum("hvr,hra->hva", parent, mats, precision=exact_mode)
        spread = (
            spread.reshape(parent_count, vectors, 2, RANK)
            .transpose(0, 2, 1, 3)
            .reshape(2 * parent_count, vectors, RANK)
        )
        level_locals[pos] = level_locals[pos] + spread
    far_part = jnp.einsum("kvr,krd->kvd", level_locals[0], leaf_basis, precision=exact_mode)
    total = far_part + NEAR_WEIGHT * near
    return total.transpose(1, 0, 2).reshape(vectors, LEAF_DEV * LEAF_PTS)


def solution(mesh):
    placed = (
        P("vec", ("parts", "leaf", "sub")),
        P(None, ("parts", "leaf", "sub")),
        P(("parts", "leaf", "sub"), None),
        P(("parts", "leaf", "sub"), None),
        P(("parts", "leaf", "sub"), None, None),
        P(("parts", "leaf", "sub"), None, None),
        P("parts", None, None),
        P("parts", None, None),
        P("parts", None, None),
    )
    return jax.shard_map(
        on_device,
        mesh=mesh,
        in_specs=placed,
        out_specs=P("vec", ("parts", "leaf", "sub")),
        check_vma=False,
    )
```

profile of v0, /device:TPU:1, one launch (start us, length us, event | category | flops | bytes accessed | tf_op | source)
XLA Modules:
  0.0 295.5 jit_solution(3466344983705164137)
XLA Ops:
  1.6 3.9 %constant_dynamic-update-slice_fusion.4 = (f32[63,32,64]{2,1,0:T(8,128)}, f32[32,32,64]{2,1,0:T(8,128)S(1)}) fusion(f32[32,64,256]{2,1,0:T(8,128)S(1)} %copy-done, f32[4,32,8,256]{3,2,1,0:T(8,128)} %bitcast.191), kind=kOutput, calls=%fused_computation.204 | convolution fusion | flops 201326592 | bytes 3932160 | tf_op jit(solution)/shard_map/kvd,krd->kvr/dot_general | solution.py:80
  8.8 2.8 constant_dynamic-update-slice_fusion.3
  27.7 2.8 copy.27
  30.5 2.4 reshape.159
  32.9 4.6 %collective-permute-start = (f32[32,4032]{1,0:T(8,128)}, f32[32,4032]{1,0:T(8,128)}, u32[]{:S(2)}, u32[]{:S(2)}) collective-permute-start(f32[32,4032]{1,0:T(8,128)} %reshape.159), channel_id=1, source_target_pairs={{0,1},{1,4},{4,5},{5,8},{8,9},{9,12},{12,13},{2,3},{3,6},{6,7},{7,... | collective-permute-start | bytes 1548296 | tf_op jit(solution)/shard_map/ppermute | solution.py:25
  40.5 3.6 %collective-permute-start.5 = (f32[32,4096]{1,0:T(8,128)}, f32[32,4096]{1,0:T(8,128)}, u32[]{:S(2)}, u32[]{:S(2)}) collective-permute-start(f32[32,4096]{1,0:T(8,128)} %get-tuple-element.94), channel_id=1, source_target_pairs={{0,1},{1,4},{4,5},{5,8},{8,9},{9,12},{12,13},{2,3},{3,6},{6,7},{7,... | collective-permute-start | bytes 1572872 | tf_op jit(solution)/shard_map/ppermute | solution.py:25
  45.7 2.4 collective-permute-start.7
  60.3 3.6 %gather_fusion.3 = f32[504,3,64]{2,1,0:T(4,128)} fusion(f32[504,3,64]{2,1,0:T(4,128)} %copy.34, s32[1024]{0:T(1024)S(1)} %get-tuple-element.152), kind=kCustom, calls=%fused_computation.3 | custom fusion | bytes 776160 | tf_op jit(solution)/shard_map/gather | solution.py:119
  75.0 2.3 collective-permute-start.4
  83.9 3.3 %collective-permute-start.8 = (f32[3,4096]{1,0:T(4,128)}, f32[3,4096]{1,0:T(4,128)S(1)}, u32[]{:S(2)}, u32[]{:S(2)}) collective-permute-start(f32[3,4096]{1,0:T(4,128)} %get-tuple-element.104), channel_id=1, source_target_pairs={{1,0},{4,1},{5,4},{8,5},{9,8},{12,9},{13,12},{3,2},{6,3},{7,6},{10... | collective-permute-start | bytes 147464 | tf_op jit(solution)/shard_map/ppermute | solution.py:26
  94.8 2.5 concatenate.36
  97.2 2.8 copy.28
  100.0 2.5 concatenate.37
  104.3 3.6 %maximum_bitcast_fusion = f32[189,32,64]{2,1,0:T(8,128)} fusion(f32[32,63,64]{2,0,1:T(8,128)S(1)} %copy.29, f32[32,63,64]{2,0,1:T(8,128)} %bitcast.196, f32[32,63,64]{2,0,1:T(8,128)} %copy.28), kind=kLoop, calls=%fused_computation.62 | loop fusion | flops 774144 | bytes 3096576 | tf_op jit(solution)/shard_map/transpose | solution.py:114
  107.9 6.2 %gather_fusion.2 = f32[504,32,64]{2,1,0:T(8,128)} fusion(f32[189,32,64]{2,1,0:T(8,128)} %maximum_bitcast_fusion, s32[1024]{0:T(1024)S(1)} %get-tuple-element.153), kind=kCustom, calls=%fused_computation.2 | custom fusion | bytes 8259552 | tf_op jit(solution)/shard_map/gather | solution.py:118
  114.2 23.7 %fusion.53 = f32[63,32,64]{2,1,0:T(8,128)S(1)} fusion(f32[63,8,64]{2,1,0:T(8,128)} %get-tuple-element.98, f32[63,64]{1,0:T(8,128)S(1)} %copy-done.8, f32[63,8,64]{2,1,0:T(8,128)} %get-tuple-element.97, f32[63,64]{1,0:T(8,128)S(1)} %copy-done.9, f32[63,8,64]{2,1,0:T(8,128)} %get-tuple-element.96, f32[63,64]{1,0:T(8,128)S(1)} %copy-done.7, ...), kind=kOutput, calls=%fused_computation.66 | convolution fusion | flops 814399488 | bytes 5082336 | tf_op jit(solution)/shard_map/nerj,nevj->nvr/dot_general | solution.py:122
  144.0 2.6 copy.38
  146.6 144.1 %while.10 = (s32[]{:T(128)}, f32[8,4,32,256]{3,2,1,0:T(8,128)}, s32[8]{0:T(128)S(1)}, s32[32,8]{1,0:T(8,128)}, s32[]{:T(128)}, /*index=5*/f32[64,32,256]{2,1,0:T...) while((s32[]{:T(128)}, f32[8,4,32,256]{3,2,1,0:T(8,128)}, ...), condition=%wide.region_1.2_spmd, body=%wide.region_0.1_spmd.sunk | while | flops 826541312 | bytes 4032427 | solution.py:58
  150.4 2.2 gather_fusion.1
  154.1 10.5 %fusion.202 = f32[8,4,32,256]{3,2,1,0:T(8,128)} fusion(f32[8,4,32,256]{3,2,1,0:T(8,128)} %get-tuple-element.231, s32[]{:T(128)} %get-tuple-element.230, f32[4,8,256]{2,1,0:T(8,128)S(1)} %get-tuple-element.213, f32[4,256]{1,0:T(4,128)S(1)} %get-tuple-element.214, f32[4,8,256]{2,1,0:T(8,128)S(1)} %get-tuple-element.215, ...), kind=kOutput, calls=%fused_computation.25.clone.1 | convolution fusion | flops 826540032 | bytes 1290880 | tf_op jit(solution)/shard_map/while/body/eval_jaxpr/betd,bevd->bvt/dot_general | solution.py:55
  168.4 2.2 gather_fusion.1
  172.2 10.5 %fusion.202 = f32[8,4,32,256]{3,2,1,0:T(8,128)} fusion(f32[8,4,32,256]{3,2,1,0:T(8,128)} %get-tuple-element.231, s32[]{:T(128)} %get-tuple-element.230, f32[4,8,256]{2,1,0:T(8,128)S(1)} %get-tuple-element.213, f32[4,256]{1,0:T(4,128)S(1)} %get-tuple-element.214, f32[4,8,256]{2,1,0:T(8,128)S(1)} %get-tuple-element.215, ...), kind=kOutput, calls=%fused_computation.25.clone.1 | convolution fusion | flops 826540032 | bytes 1290880 | tf_op jit(solution)/shard_map/while/body/eval_jaxpr/betd,bevd->bvt/dot_general | solution.py:55
  186.5 2.2 gather_fusion.1
  190.2 10.5 %fusion.202 = f32[8,4,32,256]{3,2,1,0:T(8,128)} fusion(f32[8,4,32,256]{3,2,1,0:T(8,128)} %get-tuple-element.231, s32[]{:T(128)} %get-tuple-element.230, f32[4,8,256]{2,1,0:T(8,128)S(1)} %get-tuple-element.213, f32[4,256]{1,0:T(4,128)S(1)} %get-tuple-element.214, f32[4,8,256]{2,1,0:T(8,128)S(1)} %get-tuple-element.215, ...), kind=kOutput, calls=%fused_computation.25.clone.1 | convolution fusion | flops 826540032 | bytes 1290880 | tf_op jit(solution)/shard_map/while/body/eval_jaxpr/betd,bevd->bvt/dot_general | solution.py:55
  204.5 2.2 gather_fusion.1
  208.3 10.5 %fusion.202 = f32[8,4,32,256]{3,2,1,0:T(8,128)} fusion(f32[8,4,32,256]{3,2,1,0:T(8,128)} %get-tuple-element.231, s32[]{:T(128)} %get-tuple-element.230, f32[4,8,256]{2,1,0:T(8,128)S(1)} %get-tuple-element.213, f32[4,256]{1,0:T(4,128)S(1)} %get-tuple-element.214, f32[4,8,256]{2,1,0:T(8,128)S(1)} %get-tuple-element.215, ...), kind=kOutput, calls=%fused_computation.25.clone.1 | convolution fusion | flops 826540032 | bytes 1290880 | tf_op jit(solution)/shard_map/while/body/eval_jaxpr/betd,bevd->bvt/dot_general | solution.py:55
  222.6 2.2 gather_fusion.1
  226.3 10.5 %fusion.202 = f32[8,4,32,256]{3,2,1,0:T(8,128)} fusion(f32[8,4,32,256]{3,2,1,0:T(8,128)} %get-tuple-element.231, s32[]{:T(128)} %get-tuple-element.230, f32[4,8,256]{2,1,0:T(8,128)S(1)} %get-tuple-element.213, f32[4,256]{1,0:T(4,128)S(1)} %get-tuple-element.214, f32[4,8,256]{2,1,0:T(8,128)S(1)} %get-tuple-element.215, ...), kind=kOutput, calls=%fused_computation.25.clone.1 | convolution fusion | flops 826540032 | bytes 1290880 | tf_op jit(solution)/shard_map/while/body/eval_jaxpr/betd,bevd->bvt/dot_general | solution.py:55
  244.4 10.5 %fusion.202 = f32[8,4,32,256]{3,2,1,0:T(8,128)} fusion(f32[8,4,32,256]{3,2,1,0:T(8,128)} %get-tuple-element.231, s32[]{:T(128)} %get-tuple-element.230, f32[4,8,256]{2,1,0:T(8,128)S(1)} %get-tuple-element.213, f32[4,256]{1,0:T(4,128)S(1)} %get-tuple-element.214, f32[4,8,256]{2,1,0:T(8,128)S(1)} %get-tuple-element.215, ...), kind=kOutput, calls=%fused_computation.25.clone.1 | convolution fusion | flops 826540032 | bytes 1290880 | tf_op jit(solution)/shard_map/while/body/eval_jaxpr/betd,bevd->bvt/dot_general | solution.py:55
  262.3 10.5 %fusion.202 = f32[8,4,32,256]{3,2,1,0:T(8,128)} fusion(f32[8,4,32,256]{3,2,1,0:T(8,128)} %get-tuple-element.231, s32[]{:T(128)} %get-tuple-element.230, f32[4,8,256]{2,1,0:T(8,128)S(1)} %get-tuple-element.213, f32[4,256]{1,0:T(4,128)S(1)} %get-tuple-element.214, f32[4,8,256]{2,1,0:T(8,128)S(1)} %get-tuple-element.215, ...), kind=kOutput, calls=%fused_computation.25.clone.1 | convolution fusion | flops 826540032 | bytes 1290880 | tf_op jit(solution)/shard_map/while/body/eval_jaxpr/betd,bevd->bvt/dot_general | solution.py:55
  280.3 10.5 %fusion.202 = f32[8,4,32,256]{3,2,1,0:T(8,128)} fusion(f32[8,4,32,256]{3,2,1,0:T(8,128)} %get-tuple-element.231, s32[]{:T(128)} %get-tuple-element.230, f32[4,8,256]{2,1,0:T(8,128)S(1)} %get-tuple-element.213, f32[4,256]{1,0:T(4,128)S(1)} %get-tuple-element.214, f32[4,8,256]{2,1,0:T(8,128)S(1)} %get-tuple-element.215, ...), kind=kOutput, calls=%fused_computation.25.clone.1 | convolution fusion | flops 826540032 | bytes 1290880 | tf_op jit(solution)/shard_map/while/body/eval_jaxpr/betd,bevd->bvt/dot_general | solution.py:55
  292.1 2.4 fusion.52
  (202 shorter events, 108.5 us)
Async XLA Ops:
  0.0 1.6 copy-start
  0.0 39.5 %copy-start.1 = (f32[32,8192]{1,0:T(8,128)S(1)}, f32[32,8192]{1,0:T(8,128)}, u32[]{:S(2)}) copy-start(f32[32,8192]{1,0:T(8,128)} %param.11) | copy-start | bytes 3145732
  1.6 53.0 %copy-start.3 = (f32[504,3,64]{0,2,1:T(8,128)S(1)}, f32[504,3,64]{0,2,1:T(8,128)}, u32[]{:S(2)}) copy-start(f32[504,3,64]{0,2,1:T(8,128)} %param.17) | copy-start | bytes 1161220
  32.9 61.9 %collective-permute-start = (f32[32,4032]{1,0:T(8,128)}, f32[32,4032]{1,0:T(8,128)}, u32[]{:S(2)}, u32[]{:S(2)}) collective-permute-start(f32[32,4032]{1,0:T(8,128)} %reshape.159), channel_id=1, source_target_pairs={{0,1},{1,4},{4,5},{5,8},{8,9},{9,12},{12,13},{2,3},{3,6},{6,7},{7,... | collective-permute-start | bytes 1548296 | tf_op jit(solution)/shard_map/ppermute | solution.py:25
  37.4 62.6 %collective-permute-start.1 = (f32[32,4032]{1,0:T(8,128)}, f32[32,4032]{1,0:T(8,128)}, u32[]{:S(2)}, u32[]{:S(2)}) collective-permute-start(f32[32,4032]{1,0:T(8,128)} %reshape.159), channel_id=1, source_target_pairs={{1,0},{4,1},{5,4},{8,5},{9,8},{12,9},{13,12},{3,2},{6,3},{7,6},{10... | collective-permute-start | bytes 1548296 | tf_op jit(solution)/shard_map/ppermute | solution.py:26
  39.4 28.1 %collective-permute-start.2 = (f32[32,64]{1,0:T(8,128)}, f32[32,64]{1,0:T(8,128)}, u32[]{:S(2)}, u32[]{:S(2)}) collective-permute-start(f32[32,64]{1,0:T(8,128)} %get-tuple-element.145), channel_id=1, source_target_pairs={{0,1},{1,0},{4,5},{5,4},{8,9},{9,8},{12,13},{13,12},{2,3},{3,2},{6... | collective-permute-start | bytes 24584 | tf_op jit(solution)/shard_map/ppermute | solution.py:34
  40.5 101.4 %collective-permute-start.5 = (f32[32,4096]{1,0:T(8,128)}, f32[32,4096]{1,0:T(8,128)}, u32[]{:S(2)}, u32[]{:S(2)}) collective-permute-start(f32[32,4096]{1,0:T(8,128)} %get-tuple-element.94), channel_id=1, source_target_pairs={{0,1},{1,4},{4,5},{5,8},{8,9},{9,12},{12,13},{2,3},{3,6},{6,7},{7,... | collective-permute-start | bytes 1572872 | tf_op jit(solution)/shard_map/ppermute | solution.py:25
  45.7 46.0 %collective-permute-start.7 = (f32[3,4096]{1,0:T(4,128)}, f32[3,4096]{1,0:T(4,128)}, u32[]{:S(2)}, u32[]{:S(2)}) collective-permute-start(f32[3,4096]{1,0:T(4,128)} %get-tuple-element.103), channel_id=1, source_target_pairs={{0,1},{1,4},{4,5},{5,8},{8,9},{9,12},{12,13},{2,3},{3,6},{6,7},{7,... | collective-permute-start | bytes 147464 | tf_op jit(solution)/shard_map/ppermute | solution.py:25
  69.8 2.9 collective-permute-start.3
  75.0 8.9 %collective-permute-start.4 = (f32[32,64]{1,0:T(8,128)}, f32[32,64]{1,0:T(8,128)}, u32[]{:S(2)}, u32[]{:S(2)}) collective-permute-start(f32[32,64]{1,0:T(8,128)} %fusion.82), channel_id=1, source_target_pairs={{0,8},{1,9},{4,12},{5,13},{8,0},{9,1},{12,4},{13,5},{2,10},{3,11},... | collective-permute-start | bytes 24584 | tf_op jit(solution)/shard_map/ppermute | solution.py:34
  83.9 9.9 %collective-permute-start.8 = (f32[3,4096]{1,0:T(4,128)}, f32[3,4096]{1,0:T(4,128)S(1)}, u32[]{:S(2)}, u32[]{:S(2)}) collective-permute-start(f32[3,4096]{1,0:T(4,128)} %get-tuple-element.104), channel_id=1, source_target_pairs={{1,0},{4,1},{5,4},{8,5},{9,8},{12,9},{13,12},{3,2},{6,3},{7,6},{10... | collective-permute-start | bytes 147464 | tf_op jit(solution)/shard_map/ppermute | solution.py:26
  91.7 50.3 %collective-permute-start.6 = (f32[32,4096]{1,0:T(8,128)}, f32[32,4096]{1,0:T(8,128)}, u32[]{:S(2)}, u32[]{:S(2)}) collective-permute-start(f32[32,4096]{1,0:T(8,128)} %get-tuple-element.95), channel_id=1, source_target_pairs={{1,0},{4,1},{5,4},{8,5},{9,8},{12,9},{13,12},{3,2},{6,3},{7,6},{10... | collective-permute-start | bytes 1572872 | tf_op jit(solution)/shard_map/ppermute | solution.py:26
  107.9 6.2 %copy-start.6 = (f32[63,8]{1,0:T(8,128)S(1)}, f32[63,8]{1,0:T(8,128)}, u32[]{:S(2)}) copy-start(f32[63,8]{1,0:T(8,128)} %copy.31) | copy-start | bytes 6052
  107.9 6.2 %copy-start.7 = (f32[63,64]{1,0:T(8,128)S(1)}, f32[63,64]{1,0:T(8,128)}, u32[]{:S(2)}) copy-start(f32[63,64]{1,0:T(8,128)} %get-tuple-element.105) | copy-start | bytes 48388
  107.9 6.2 %copy-start.8 = (f32[63,64]{1,0:T(8,128)S(1)}, f32[63,64]{1,0:T(8,128)}, u32[]{:S(2)}) copy-start(f32[63,64]{1,0:T(8,128)} %get-tuple-element.106) | copy-start | bytes 48388
  107.9 6.2 %copy-start.9 = (f32[63,64]{1,0:T(8,128)S(1)}, f32[63,64]{1,0:T(8,128)}, u32[]{:S(2)}) copy-start(f32[63,64]{1,0:T(8,128)} %get-tuple-element.107) | copy-start | bytes 48388
  114.1 23.8 %copy-start.10 = (f32[32,128]{1,0:T(8,128)S(1)}, f32[32,128]{1,0:T(8,128)}, u32[]{:S(2)}) copy-start(f32[32,128]{1,0:T(8,128)} %fusion.84) | copy-start | bytes 49156
  114.1 23.8 %copy-start.11 = (f32[64]{0:T(128)S(1)}, f32[64]{0:T(128)}, u32[]{:S(2)}) copy-start(f32[64]{0:T(128)} %get-tuple-element.67) | copy-start | bytes 772
  114.1 23.8 %copy-start.12 = (f32[64]{0:T(128)S(1)}, f32[64]{0:T(128)}, u32[]{:S(2)}) copy-start(f32[64]{0:T(128)} %get-tuple-element.68) | copy-start | bytes 772
  114.2 23.8 %copy-start.13 = (f32[64]{0:T(128)S(1)}, f32[64]{0:T(128)}, u32[]{:S(2)}) copy-start(f32[64]{0:T(128)} %get-tuple-element.69) | copy-start | bytes 772
  114.2 24.8 %copy-start.5 = (f32[128,64]{1,0:T(8,128)S(1)}, f32[128,64]{1,0:T(8,128)}, u32[]{:S(2)}) copy-start(f32[128,64]{1,0:T(8,128)} %copy.36) | copy-start | bytes 98308
  114.2 25.1 %copy-start.2 = (f32[31,64,128]{2,1,0:T(8,128)S(1)}, f32[31,64,128]{2,1,0:T(8,128)}, u32[]{:S(2)}) copy-start(f32[31,64,128]{2,1,0:T(8,128)} %param.16) | copy-start | bytes 3047428
  137.9 4.1 %copy-start.4 = (f32[63,32,64]{2,1,0:T(8,128)}, f32[63,32,64]{2,1,0:T(8,128)S(1)}, u32[]{:S(2)}) copy-start(f32[63,32,64]{2,1,0:T(8,128)S(1)} %fusion.53) | copy-start | bytes 1548292
  140.3 6.2 %copy-start.14 = (s32[8]{0:T(128)S(1)}, s32[8]{0:T(128)}, u32[]{:S(2)}) copy-start(s32[8]{0:T(128)} %iota_multiply_fusion) | copy-start | bytes 100
where the time goes:
time: 299 us; the launch traced here: 296 us
  matrix products  134 us (45%)
  local copies, waits for them, and re-layouts  101 us (34%)
  other arithmetic  23.6 us (8%)
  starting transfers between devices  21.6 us (7%)
  loops' own time  13.8 us (5%)
    dot_general x8, matrix products, near_block(): jnp.einsum('betd,bevd->bvt', tiles, source_charges, precision=exact_mode)  83.8 us
    dot_general x1, matrix products, on_device(): far = jnp.einsum('nerj,nevj->nvr', tiles, source_coef, precision=exact_mode)  23.7 us
    gather x8, local copies, waits for them, and re-layouts, near_block(): source_charges = source_charges_all[picked] * valid[:, :, None, None]  17.6 us
    another operation x1, loops' own time, near_field(): result = lax.map(near_block, block_starts)  13.8 us
    ppermute x3, starting transfers between devices, with_halo(): before = lax.ppermute(last, axis, up)  10.6 us
    dot_general x5, matrix products, on_device(): current = jnp.einsum('hva,hra->hvr', paired, mats, precision=exact_mode)  10.1 us
    concatenate x4, local copies, waits for them, and re-layouts, with_halo(): shard = jnp.concatenate([before, shard, after], axis=dim)  9.52 us
    ppermute x3, starting transfers between devices, with_halo(): after = lax.ppermute(first, axis, down)  7.36 us
  transfers between devices with their start and end apart: 9, of which 1 were waited for; matrix products, arithmetic and copies ran while one was open for 29% of the time, Pallas kernels for 0%

commit v1 on v0

v1 whole, which is shorter than its diff:
```python
import functools

import jax
import jax.numpy as jnp
import numpy as np
from jax import lax
from jax.experimental import pallas as pl
from jax.experimental.pallas import tpu as pltpu
from jax.sharding import PartitionSpec as P

PTS = 256
RANK = 64
LEAVES = 32
NODES = 63
SLOTS = 8
REACH = 16
HALF = REACH * PTS
ROWS = 8
PAD = 16
GROUP = 4
WIDTH = 0.05
NEAR_WEIGHT = 0.0625
EMPTY = 3 * 64
F32 = jnp.float32
BF16 = jnp.bfloat16
AXES = ("leaf", "sub")
NN = (((1,), (0,)), ((), ()))
NT = (((1,), (1,)), ((), ()))
TN = (((0,), (0,)), ((), ()))


def selections():
    source_part = (1, 1, 2, 2, 1, 3)
    target_part = (1, 2, 1, 2, 3, 1)
    source = np.zeros((64, 32), np.float32)
    target = np.zeros((32, 64), np.float32)
    for g in range(6):
        for c in range(3):
            source[(source_part[g] - 1) * 8 + c, 4 * g + c] = 1
            target[4 * g + c, (target_part[g] - 1) * 8 + c] = -2
        f = 4 * g + 3
        if g < 3:
            source[24 + 8 * g, f] = 1
            target[f, 48] = 1
        else:
            source[48, f] = 1
            target[f, 24 + 8 * (g - 3)] = 1
    source[48, 24] = 1
    target[24, 48] = 1
    wide = np.zeros((64, 256), np.float32)
    wide[:, :32] = source
    wide[:, 128 + 32 : 128 + 64] = source
    return jnp.asarray(wide, BF16), jnp.asarray(target, BF16)


def halves(x):
    high = x.astype(BF16)
    return high, (x - high.astype(F32)).astype(BF16)


def dot(a, b, dims=NN):
    return lax.dot_general(a, b, dims, preferred_element_type=F32)


def dot3(a, b, dims=NN):
    ah, al = halves(a)
    bh, bl = halves(b)
    rows = a.shape[0]
    both = dot(jnp.concatenate([ah, al], axis=0), bh, dims)
    return both[:rows] + both[rows:] + dot(ah, bl, dims)


def parts_of(points):
    n = points.shape[1]
    c = (points - 0.5) * (1.0 / WIDTH)
    c = jnp.concatenate([c, jnp.zeros((5, n), F32)], axis=0)

    def rounded(x):
        return x.astype(BF16).astype(F32)

    p1 = rounded(c)
    rest = c - p1
    p2 = rounded(rest)
    p3 = rest - p2
    norm = jnp.broadcast_to(jnp.sum(c * c, axis=0, keepdims=True), (8, n))
    n1 = rounded(norm)
    rest = norm - n1
    n2 = rounded(rest)
    n3 = rest - n2
    rows = [p1, p2, p3, n1, n2, n3, jnp.ones((8, n), F32), jnp.zeros((8, n), F32)]
    return jnp.concatenate(rows, axis=0).astype(BF16)


def lower_lanes(rows):
    return lax.broadcasted_iota(jnp.int32, (rows, 128), 1) < RANK


def diagonal(x, vectors):
    return jnp.where(lower_lanes(vectors), x[:vectors], x[vectors:])


def spread_pair(pair):
    low = lower_lanes(pair.shape[0])
    zero = jnp.zeros_like(pair)
    return jnp.concatenate([jnp.where(low, pair, zero), jnp.where(low, zero, pair)], axis=0)


def pipelined(steps, first, second):
    for u in range(GROUP):
        first(u, u, 0)

    def body(i, carry):
        for h in range(2):
            base = (2 * i + h) * GROUP
            for u in range(GROUP):
                first(base + GROUP + u, u, 1 - h)
            for u in range(GROUP):
                second(base + u, u, h)
        return carry

    lax.fori_loop(0, (steps + 2 * GROUP - 1) // (2 * GROUP), body, 0)


def up_kernel(
    near_ref, far_ref, far_vec, charges_hbm, coords_hbm, basis_hbm, transfer_hbm,
    up_ref, down_ref, root_ref, local_ref, halo_ref, steps_ref, count_ref, entry_ref,
    charges, coords, basis, transfer, coef, sems,
):
    vectors = charges.shape[0]
    copies = [
        pltpu.make_async_copy(charges_hbm, charges, sems.at[0]),
        pltpu.make_async_copy(basis_hbm, basis, sems.at[1]),
        pltpu.make_async_copy(transfer_hbm, transfer, sems.at[2]),
        pltpu.make_async_copy(coords_hbm, coords, sems.at[3]),
    ]
    for copy in copies:
        copy.start()
    device = lax.axis_index(AXES)
    first = device * LEAVES

    def scan_leaf(t, counts):
        here, there = counts
        for e in range(SLOTS):
            entry = near_ref[t, e]
            s = entry - first
            inside = jnp.logical_and(s >= 0, s < LEAVES)
            outside = jnp.logical_and(entry >= 0, jnp.logical_not(inside))
            local_ref[here] = t * 256 + s
            halo_ref[there] = t * 256 + jnp.where(s < 0, s + REACH, s - REACH)
            here = here + inside.astype(jnp.int32)
            there = there + outside.astype(jnp.int32)
        return here, there

    here, there = lax.fori_loop(0, LEAVES, scan_leaf, (jnp.int32(0), jnp.int32(0)))
    for u in range(PAD):
        local_ref[here + u] = LEAVES
        halo_ref[there + u] = LEAVES
    for p in range(32):
        steps_ref[p] = p * 256 + 2 * p

    def scan_pair(p, count):
        top = far_ref[2 * p, 4]
        for e in range(4):
            for c in range(2):
                top = jnp.maximum(top, far_ref[jnp.minimum(2 * p + c, NODES - 1), 4 + e])
        steps_ref[count] = p * 256 + 2 * p + 1
        return count + (top >= 0).astype(jnp.int32)

    total = lax.fori_loop(0, 32, scan_pair, jnp.int32(32))
    for u in range(PAD):
        steps_ref[total + u] = 32 * 256
    count_ref[0] = here
    count_ref[1] = there
    count_ref[2] = total
    entry = far_vec[...]
    place = entry - (device - 1) * NODES
    place = place + (place >= NODES).astype(jnp.int32) + (place >= 2 * NODES).astype(jnp.int32)
    place = jnp.where(entry >= 0, place, EMPTY)
    entry_ref[0:NODES] = place
    entry_ref[NODES:64] = jnp.full((1, SLOTS), EMPTY, jnp.int32)

    copies[0].wait()
    copies[1].wait()

    def put(pair, value):
        coef[pair] = value

    for p in range(LEAVES // 2):
        a, b = slice(2 * p * PTS, (2 * p + 1) * PTS), slice((2 * p + 1) * PTS, (2 * p + 2) * PTS)
        both = jnp.concatenate([charges[:, a], charges[:, b]], axis=0)
        put(p, diagonal(dot3(both, basis[2 * p : 2 * p + 2].reshape(2 * RANK, PTS), NT), vectors))
    copies[2].wait()
    for p in range(LEAVES // 2, LEAVES - 1):
        q = 2 * p - LEAVES
        both = coef[q : q + 2].reshape(2 * vectors, 128)
        put(p, diagonal(dot3(both, transfer[q : q + 2].reshape(128, 128), NT), vectors))
    root = dot3(coef[30], transfer[30], NT)
    root = jnp.concatenate([root, jnp.zeros((vectors, RANK), F32)], axis=1)
    put(31, root)
    root_ref[...] = root
    copies[3].wait()
    up_ref[0:vectors] = charges[:, HALF:]
    down_ref[0:vectors] = charges[:, :HALF]
    for p in range(LEAVES):
        lanes = slice(p * 128, (p + 1) * 128)
        up_ref[vectors : 2 * vectors, lanes] = coef[p]
        down_ref[vectors : 2 * vectors, lanes] = coef[p]
    up_ref[2 * vectors : 2 * vectors + 3] = coords[:, HALF:]
    down_ref[2 * vectors : 2 * vectors + 3] = coords[:, :HALF]
    up_ref[2 * vectors + 3 :] = jnp.zeros((5, HALF), F32)
    down_ref[2 * vectors + 3 :] = jnp.zeros((5, HALF), F32)


def source_tables(k, charges, points, select, sources, weights):
    parts = parts_of(points)
    sources[k] = dot(parts, select[:, 0:32], TN).astype(BF16)
    high, low = halves(charges)
    weights[k] = jnp.concatenate([high, low], axis=0)
    return parts


def near_steps(list_ref, sources, targets, weights, out_ref, tiles):
    vectors = out_ref.shape[0]
    highs = (tiles[:GROUP], tiles[GROUP : 2 * GROUP])
    lows = (tiles[2 * GROUP : 3 * GROUP], tiles[3 * GROUP :])

    def decode(j):
        code = list_ref[j]
        return lax.shift_right_logical(code, 8), jnp.bitwise_and(code, 255)

    def first(j, u, b):
        t, s = decode(j)
        high, low = halves(lax.rsqrt(dot(sources[s], targets[t])))
        highs[b][u][...] = high
        lows[b][u][...] = low

    def second(j, u, b):
        t, s = decode(j)
        q = weights[s]
        both = dot(q, highs[b][u][...])
        lanes = pl.ds(pl.multiple_of(t * PTS, PTS), PTS)
        out_ref[:, lanes] += both[:vectors] + both[vectors:] + dot(q[:vectors], lows[b][u][...])

    return first, second


def near_kernel(
    count_ref, list_ref, charges, coords, select, select_t,
    near_ref, targets_ref, sources, weights, *tiles,
):
    vectors = charges.shape[0]
    for k in range(LEAVES):
        lanes = slice(k * PTS, (k + 1) * PTS)
        parts = source_tables(k, charges[:, lanes], coords[:, lanes], select, sources, weights)
        targets_ref[k] = dot(select_t[...], parts).astype(BF16)
    weights[LEAVES] = jnp.zeros((2 * vectors, PTS), BF16)
    sources[LEAVES] = sources[0]
    near_ref[...] = jnp.zeros_like(near_ref)
    first, second = near_steps(list_ref, sources, targets_ref, weights, near_ref, tiles)
    pipelined(count_ref[0], first, second)


def down_kernel(
    groups, count_ref, list_ref, steps_ref, entry_ref,
    near, targets, lower, own, upper, roots, basis, transfer,
    skel0, skel1, skel2, top_transfer, top_skeleton, select, select_t,
    out_ref,
    sources, weights, skel_points, skel_even, skel_odd, skel_targets,
    coef_low, coef_high, local, top_coef, *tiles,
):
    vectors = near.shape[0]
    device = lax.axis_index(AXES)
    low_mask = lower_lanes(vectors)
    for k in range(LEAVES):
        buffer = lower if k < REACH else upper
        lanes = slice((k % REACH) * PTS, (k % REACH + 1) * PTS)
        source_tables(
            k, buffer[0:vectors, lanes], buffer[2 * vectors : 2 * vectors + 3, lanes],
            select, sources, weights,
        )
    weights[LEAVES] = jnp.zeros((2 * vectors, PTS), BF16)
    sources[LEAVES] = sources[0]
    out_ref[...] = near[...]
    first, second = near_steps(list_ref, sources, targets, weights, out_ref, tiles)
    pipelined(count_ref[1], first, second)

    for b, skel in enumerate((skel0, skel1, skel2)):
        for p in range(32):
            left = skel[2 * p]
            right = skel[2 * p + 1] if p < 31 else jnp.zeros((3, RANK), F32)
            skel_points[b, :, p * 128 : (p + 1) * 128] = jnp.concatenate([left, right], axis=1)
        for g in range(8):
            lanes = slice(g * 512, (g + 1) * 512)
            parts = parts_of(skel_points[b, :, lanes])
            feature = dot(parts, select[...], TN).astype(BF16).reshape(8, RANK, 256)
            skel_even[b * 64 + g * 8 : b * 64 + (g + 1) * 8] = feature[:, :, 0:RANK]
            skel_odd[b * 64 + g * 8 : b * 64 + (g + 1) * 8] = feature[:, :, 128 : 128 + RANK]
            if b == 1:
                target = dot(select_t[...], parts)
                for u in range(4):
                    skel_targets[g * 4 + u] = spread_pair(target[:, u * 128 : (u + 1) * 128]).astype(BF16)
    skel_even[EMPTY] = skel_even[0]
    skel_odd[EMPTY] = skel_odd[0]
    for b, buffer in enumerate((lower, own, upper)):
        for p in range(32):
            pair = buffer[vectors : 2 * vectors, p * 128 : (p + 1) * 128]
            swap = pltpu.roll(pair, RANK, 1)
            zero = jnp.zeros_like(pair)
            for n, (a, c) in enumerate(((pair, swap), (swap, pair))):
                for table, value in (
                    (coef_low, jnp.where(low_mask, a, zero)),
                    (coef_high, jnp.where(low_mask, zero, c)),
                ):
                    high, low = halves(value)
                    table[b * 64 + 2 * p + n] = jnp.concatenate([high, low], axis=0)
    coef_low[EMPTY] = jnp.zeros((2 * vectors, 128), BF16)
    coef_high[EMPTY] = jnp.zeros((2 * vectors, 128), BF16)
    local[...] = jnp.zeros_like(local)

    far_highs = (tiles[:GROUP], tiles[GROUP : 2 * GROUP])
    far_lows = (tiles[2 * GROUP : 3 * GROUP], tiles[3 * GROUP :])

    def entries(j):
        code = steps_ref[j]
        target = lax.shift_right_logical(code, 8)
        chunk = jnp.bitwise_and(code, 255)
        p = lax.shift_right_logical(chunk, 1)
        slot = 4 * jnp.bitwise_and(chunk, 1)
        even = [entry_ref[2 * p, slot + e] for e in range(4)]
        odd = [entry_ref[2 * p + 1, slot + e] for e in range(4)]
        return target, p, even, odd

    def far_first(j, u, b):
        target, p, even, odd = entries(j)
        rows = [skel_even[even[e]] + skel_odd[odd[e]] for e in range(4)]
        x = dot(jnp.concatenate(rows, axis=0), skel_targets[p])
        high, low = halves(lax.rsqrt(x))
        far_highs[b][u][:, 0:128] = high
        far_lows[b][u][:, 0:128] = low

    def far_second(j, u, b):
        target, p, even, odd = entries(j)

        def side(s):
            return jnp.concatenate(
                [coef_low[s[0]] + coef_high[s[1]], coef_low[s[2]] + coef_high[s[3]]], axis=1
            )

        sides = (side(even), side(odd))
        empty = jnp.logical_or(target == 32, False)
        stack = jnp.concatenate(
            [sides[0][:vectors], sides[1][:vectors], sides[0][vectors:], sides[1][vectors:]], axis=0
        )
        both = dot(stack, far_highs[b][u][:, 0:128])
        total = both[: 2 * vectors] + both[2 * vectors :]
        total = total + dot(stack[: 2 * vectors], far_lows[b][u][:, 0:128])
        local[target] += diagonal(total, vectors)

    pipelined(count_ref[2], far_first, far_second)

    bits = groups.bit_length() - 1
    offsets = []
    offset = 0
    for h in range(bits):
        count = groups >> h
        offsets.append(offset)
        for i in range(count // 2):
            if h == 0:
                pair = roots[2 * i] + pltpu.roll(roots[2 * i + 1], RANK, 1)
            else:
                start = groups - (groups >> (h - 1)) + 2 * i
                below = offsets[h - 1] + 2 * i
                both = top_coef[below : below + 2].reshape(2 * vectors, 128)
                matrix = top_transfer[start : start + 2].reshape(128, 128)
                pair = diagonal(dot3(both, matrix, NT), vectors)
            top_coef[offset + i] = pair
        offset += count // 2
    row = lax.broadcasted_iota(jnp.int32, (128, 128), 0) < RANK
    lane = lax.broadcasted_iota(jnp.int32, (128, 128), 1) < RANK
    couple = []
    for h in range(bits):
        node = device // 2**h
        i = node // 2
        if h == 0:
            odd = node % 2 == 1
            left = jnp.where(odd, skel0[NODES - 1], skel1[NODES - 1])
            right = jnp.where(odd, skel1[NODES - 1], skel2[NODES - 1])
        else:
            start = groups - (groups >> (h - 1))
            left = top_skeleton[start + 2 * i]
            right = top_skeleton[start + 2 * i + 1]
        parts = parts_of(jnp.concatenate([left, right], axis=1))
        feature = dot(parts, select[:, 0:32], TN).astype(BF16)
        target = dot(select_t[...], parts).astype(BF16)
        tile = jnp.where(row != lane, lax.rsqrt(dot(feature, target)), 0.0)
        couple.append(dot3(top_coef[offsets[h] + i], tile))
    top = couple[bits - 1]
    for h in range(bits - 2, -1, -1):
        parent = device // 2 ** (h + 1)
        mine = jnp.where(low_mask == (parent % 2 == 0), top, 0.0)
        start = groups - (groups >> h) + 2 * (parent // 2)
        matrix = top_transfer[pl.ds(start, 2)].reshape(128, 128)
        top = couple[h] + dot3(mine, matrix)
    top = jnp.where(device % 2 == 1, pltpu.roll(top, RANK, 1), top)

    local[30] += dot3(jnp.where(low_mask, local[31] + top, 0.0)[:, :RANK], transfer[30])
    for p in range(30, 15, -1):
        q = 2 * p - LEAVES
        both = dot3(spread_pair(local[p]), transfer[q : q + 2].reshape(128, 128))
        local[q] += both[:vectors]
        local[q + 1] += both[vectors:]
    for p in range(LEAVES // 2):
        both = dot3(spread_pair(local[p]), basis[2 * p : 2 * p + 2].reshape(128, PTS))
        for c in range(2):
            lanes = slice((2 * p + c) * PTS, (2 * p + c + 1) * PTS)
            out_ref[:, lanes] = both[c * vectors : (c + 1) * vectors] + NEAR_WEIGHT * out_ref[:, lanes]


def whole(count, space=pltpu.VMEM):
    return [pl.BlockSpec(memory_space=space)] * count


def on_device(
    charges, coordinates, near_lists, far_lists, leaf_basis, local_transfer,
    skeleton, top_transfer, top_skeleton,
):
    vectors = charges.shape[0]
    groups = lax.axis_size(AXES)
    points = LEAVES * PTS
    height = 2 * vectors + ROWS
    shape = jax.ShapeDtypeStruct
    select, select_t = selections()
    params = pltpu.CompilerParams(vmem_limit_bytes=56 << 20)
    smem = pltpu.SMEM
    up, down, root, local_list, halo_list, steps, counts, entries = pl.pallas_call(
        up_kernel,
        out_shape=[
            shape((height, HALF), F32),
            shape((height, HALF), F32),
            shape((vectors, 128), F32),
            shape((LEAVES * SLOTS + PAD,), jnp.int32),
            shape((LEAVES * SLOTS + PAD,), jnp.int32),
            shape((64 + PAD,), jnp.int32),
            shape((3,), jnp.int32),
            shape((64, SLOTS), jnp.int32),
        ],
        in_specs=whole(2, smem) + whole(1) + whole(4, pl.ANY),
        out_specs=whole(3) + whole(4, smem) + whole(1),
        scratch_shapes=[
            pltpu.VMEM((vectors, points), F32),
            pltpu.VMEM((3, points), F32),
            pltpu.VMEM((LEAVES, RANK, PTS), F32),
            pltpu.VMEM((LEAVES - 1, RANK, 128), F32),
            pltpu.VMEM((LEAVES, vectors, 128), F32),
            pltpu.SemaphoreType.DMA((4,)),
        ],
        compiler_params=params,
    )(near_lists, far_lists, far_lists, charges, coordinates, leaf_basis, local_transfer)

    upward = [(i, i + 1) for i in range(groups - 1)]
    lower = lax.ppermute(up, AXES, upward)
    upper = lax.ppermute(down, AXES, [(j, i) for i, j in upward])
    roots = lax.all_gather(root, AXES)

    tiles = [pltpu.VMEM((PTS, PTS), BF16)] * (4 * GROUP)
    near, targets = pl.pallas_call(
        near_kernel,
        out_shape=[shape((vectors, points), F32), shape((LEAVES, 32, PTS), BF16)],
        in_specs=whole(2, smem) + whole(4),
        out_specs=whole(2),
        scratch_shapes=[
            pltpu.VMEM((LEAVES + 1, PTS, 32), BF16),
            pltpu.VMEM((LEAVES + 1, 2 * vectors, PTS), BF16),
        ]
        + tiles,
        compiler_params=params,
        cost_estimate=pl.CostEstimate(
            flops=192 * 3 * 2 * PTS**3, transcendentals=192 * PTS**2, bytes_accessed=4 << 20
        ),
    )(counts, local_list, charges, coordinates, select, select_t)

    def block(shift):
        def index(i):
            device = lax.axis_index(AXES)
            return (jnp.clip(device + shift, 0, groups - 1), 0, 0)

        return pl.BlockSpec((NODES, 3, RANK), index)

    return pl.pallas_call(
        functools.partial(down_kernel, groups),
        out_shape=shape((vectors, points), F32),
        grid=(1,),
        in_specs=whole(4, smem)
        + whole(8)
        + [block(-1), block(0), block(1)]
        + whole(4),
        out_specs=pl.BlockSpec(memory_space=pltpu.VMEM),
        scratch_shapes=[
            pltpu.VMEM((LEAVES + 1, PTS, 32), BF16),
            pltpu.VMEM((LEAVES + 1, 2 * vectors, PTS), BF16),
            pltpu.VMEM((3, 3, HALF), F32),
            pltpu.VMEM((EMPTY + 1, RANK, RANK), BF16),
            pltpu.VMEM((EMPTY + 1, RANK, RANK), BF16),
            pltpu.VMEM((32, RANK, 128), BF16),
            pltpu.VMEM((EMPTY + 1, 2 * vectors, 128), BF16),
            pltpu.VMEM((EMPTY + 1, 2 * vectors, 128), BF16),
            pltpu.VMEM((33, vectors, 128), F32),
            pltpu.VMEM((groups, vectors, 128), F32),
        ]
        + tiles,
        compiler_params=params,
    )(
        counts, halo_list, steps, entries, near, targets, lower, up, upper, roots,
        leaf_basis, local_transfer, skeleton, skeleton, skeleton, top_transfer, top_skeleton,
        select, select_t,
    )


def solution(mesh):
    placed = (
        P("vec", ("parts", "leaf", "sub")),
        P(None, ("parts", "leaf", "sub")),
        P(("parts", "leaf", "sub"), None),
        P(("parts", "leaf", "sub"), None),
        P(("parts", "leaf", "sub"), None, None),
        P(("parts", "leaf", "sub"), None, None),
        P("parts", None, None),
        P("parts", None, None),
        P("parts", None, None),
    )
    return jax.shard_map(
        on_device,
        mesh=mesh,
        in_specs=placed,
        out_specs=P("vec", ("parts", "leaf", "sub")),
        check_vma=False,
    )
```

time: 299 us -> 82.4 us (0.28); the launches traced: 296 us -> 82.3 us
  matrix products: 134 us -> 0 us
  local copies, waits for them, and re-layouts: 101 us -> 5.49 us
  Pallas kernels: 0 us -> 47.7 us
  other arithmetic: 23.6 us -> 0 us
  blocking collectives: 0 us -> 22.6 us
  starting transfers between devices: 21.6 us -> 6.51 us
  loops' own time: 13.8 us -> 0 us
    dot_general x28 -> x0, matrix products: 134 us -> none  [the longest x8 83.8 us: near_block(): jnp.einsum('betd,bevd->bvt', tiles, source_charges, precision=exact_mode)]
    pallas_call x0 -> x3, Pallas kernels: none -> 47.7 us  [the longest x1 23.6 us: on_device(): pl.pallas_call(functools.partial(down_kernel, groups), out_shape=shape((v...]
    gather x19 -> x0, local copies, waits for them, and re-layouts: 33.8 us -> none  [the longest x8 17.6 us: near_block(): source_charges = source_charges_all[picked] * valid[:, :, None, None]]
    all_gather x0 -> x1, blocking collectives: none -> 22.6 us  [on_device(): roots = lax.all_gather(root, AXES)]
    ppermute x9 -> x2, starting transfers between devices: 21.6 us -> 6.51 us  [the longest x1 4.55 us: on_device(): lower = lax.ppermute(up, AXES, upward)]
    another operation x1 -> x0, loops' own time: 13.8 us -> none  [near_field(): result = lax.map(near_block, block_starts)]
    reshape x7 -> x0, local copies, waits for them, and re-layouts: 11.3 us -> none  [the longest x4 7.04 us: on_device(): paired = current.reshape(half, 2, vectors, RANK).transpose(0, 2, 1, 3).re...]
    concatenate x4 -> x0, local copies, waits for them, and re-layouts: 9.52 us -> none  [with_halo(): shard = jnp.concatenate([before, shard, after], axis=dim)]
  transfers between devices with their start and end apart: 9 -> 2, of which waited for: 1 -> 0; matrix products, arithmetic and copies ran while one was open for 29% -> 2% of each run, Pallas kernels for 0% -> 20%
where the time goes in v1:
time: 82.4 us; the launch traced here: 82.3 us
  Pallas kernels  47.7 us (58%)
  blocking collectives  22.6 us (27%)
  starting transfers between devices  6.51 us (8%)
  local copies, waits for them, and re-layouts  5.49 us (7%)
    pallas_call x1, Pallas kernels, on_device(): pl.pallas_call(functools.partial(down_kernel, groups), out_shape=shape((v...  23.6 us
    all_gather x1, blocking collectives, on_device(): roots = lax.all_gather(root, AXES)  22.6 us
    pallas_call x1, Pallas kernels, on_device(): pl.pallas_call(near_kernel, out_shape=[shape((vectors, points), F32), sha...  16.4 us
    pallas_call x1, Pallas kernels, on_device(): pl.pallas_call(up_kernel, out_shape=[shape((height, HALF), F32), shape((h...  7.66 us
    unnamed x11, local copies, waits for them, and re-layouts  5.49 us
    ppermute x1, starting transfers between devices, on_device(): lower = lax.ppermute(up, AXES, upward)  4.55 us
    ppermute x1, starting transfers between devices, on_device(): upper = lax.ppermute(down, AXES, [(j, i) for i, j in upward])  1.96 us
  transfers between devices with their start and end apart: 2, of which 0 were waited for; matrix products, arithmetic and copies ran while one was open for 2% of the time, Pallas kernels for 20%

profile of v1, /device:TPU:1, one launch (start us, length us, event | category | flops | bytes accessed | tf_op | source)
XLA Modules:
  0.0 82.3 jit_solution(7208738169508830804)
XLA Ops:
  0.0 1.4 %copy.12.near_ref = s32[32,8]{1,0:T(8,128)} copy(s32[32,8]{0,1:T(8,128)} %param.13) | data formatting | bytes 2048 | tf_op args[2]
  1.4 1.4 %copy.13.far_ref.far_vec = s32[63,8]{1,0:T(8,128)} copy(s32[63,8]{0,1:T(8,128)} %param.14) | data formatting | bytes 4032 | tf_op args[3]
  2.7 0.0 copy-start.2
  2.8 7.7 %shard_map.109 = (f32[72,4096]{1,0:T(8,128)}, f32[72,4096]{1,0:T(8,128)}, f32[32,128]{1,0:T(8,128)}, s32[272]{0:T(512)}, s32[272]{0:T(512)}, /*index=5*/s32[80]{0:T(128)}, s32[3]{0:T(128)}, s32[64,8]{1,0:T(8,128)}) custom-call(s32[32,8]{1,0:T(8,128)} %copy.12.near_ref, s32[63,8]{1,0:T(8,128)} %copy.13.far_ref.far_vec, s32[63,8]{1,0:T(8,128)} %copy.13.far_ref.far_vec, ...), custom_call_target="tpu_custom_call" | custom-call | tf_op jit(solution)/shard_map/pallas_call | solution.py:435
  10.4 0.0 copy-start.3
  10.4 2.0 %collective-permute-start.1 = (f32[72,4096]{1,0:T(8,128)}, f32[72,4096]{1,0:T(8,128)S(1)}, u32[]{:S(2)}, u32[]{:S(2)}) collective-permute-start(f32[72,4096]{1,0:T(8,128)} %get-tuple-element.23), channel_id=1, source_target_pairs={{1,0},{4,1},{5,4},{8,5},{9,8},{12,9},{13,12},{3,2},{6,3},{7,6},{10... | collective-permute-start | bytes 3538952 | tf_op jit(solution)/shard_map/ppermute | solution.py:462
  12.4 4.5 %collective-permute-start = (f32[72,4096]{1,0:T(8,128)}, f32[72,4096]{1,0:T(8,128)S(1)}, u32[]{:S(2)}, u32[]{:S(2)}) collective-permute-start(f32[72,4096]{1,0:T(8,128)} %get-tuple-element.22.own), channel_id=1, source_target_pairs={{0,1},{1,4},{4,5},{5,8},{8,9},{9,12},{12,13},{2,3},{3,6},{6,7},{7,... | collective-permute-start | bytes 3538952 | tf_op jit(solution)/shard_map/ppermute | solution.py:461
  17.0 0.0 copy-done.2
  17.0 1.3 %copy.15.skel0.skel1.skel2 = f32[504,3,64]{2,1,0:T(4,128)} copy(f32[504,3,64]{0,2,1:T(8,128)S(1)} %copy-done.2) | data formatting | bytes 774144 | tf_op args[6]
  18.3 0.0 copy-done.3
  18.3 22.6 %all-gather = f32[256,128]{1,0:T(8,128)} all-gather(f32[32,128]{1,0:T(8,128)S(1)} %copy-done.3), channel_id=2, replica_groups=mesh['parts'=2,'leaf'=4,'vec'=2,'sub'=2] {'leaf','sub'}, dimensions={0}, use_global_device_ids=true | all-gather | bytes 147456 | tf_op jit(solution)/shard_map/all_gather | solution.py:463
  40.9 16.4 %shard_map.110 = (f32[32,8192]{1,0:T(8,128)}, bf16[32,32,256]{2,1,0:T(8,128)(2,1)}) custom-call(s32[3]{0:T(128)} %get-tuple-element.15.count_ref, s32[272]{0:T(512)} %get-tuple-element.19.list_ref, f32[32,8192]{1,0:T(8,128)} %charges.1, f32[3,8192]{1,0:T(4,128)} %coords.1, bf16[64,256]{1,0:T(8,128)(2,1)} %constant.4.clone.select, ...), custom_call_target="tpu_custom_call" | custom-call | flops 19327352832 | bytes 4194304 | tf_op jit(solution)/shard_map/pallas_call | solution.py:466
  57.3 0.0 collective-permute-done.1.upper
  57.3 0.0 copy-start
  57.3 0.0 collective-permute-done.lower
  57.3 0.0 copy-start.1
  57.3 1.0 %copy-done = f32[72,4096]{1,0:T(8,128)} copy-done((f32[72,4096]{1,0:T(8,128)}, f32[72,4096]{1,0:T(8,128)S(1)}, u32[]{:S(2)}) %copy-start) | copy-done | bytes 1179672
  58.3 0.4 copy-done.1
  58.7 23.6 %shard_map.111 = f32[32,8192]{1,0:T(8,128)} custom-call(s32[3]{0:T(128)} %get-tuple-element.15.count_ref, s32[272]{0:T(512)} %get-tuple-element.16.list_ref, s32[80]{0:T(128)} %get-tuple-element.17.steps_ref, s32[64,8]{1,0:T(8,128)} %get-tuple-element.18.entry_ref, f32[32,8192]{1,0:T(8,128)} %get-tuple-element.20.near, ...), custom_call_target="tpu_custom_call" | custom-call | tf_op jit(solution)/shard_map/pallas_call | solution.py:489
Async XLA Ops:
  2.7 14.2 %copy-start.2 = (f32[504,3,64]{0,2,1:T(8,128)S(1)}, f32[504,3,64]{0,2,1:T(8,128)}, u32[]{:S(2)}) copy-start(f32[504,3,64]{0,2,1:T(8,128)} %param.17) | copy-start | bytes 1161220
  10.4 7.9 %copy-start.3 = (f32[32,128]{1,0:T(8,128)S(1)}, f32[32,128]{1,0:T(8,128)}, u32[]{:S(2)}) copy-start(f32[32,128]{1,0:T(8,128)} %get-tuple-element.24) | copy-start | bytes 49156
  10.4 46.8 %collective-permute-start.1 = (f32[72,4096]{1,0:T(8,128)}, f32[72,4096]{1,0:T(8,128)S(1)}, u32[]{:S(2)}, u32[]{:S(2)}) collective-permute-start(f32[72,4096]{1,0:T(8,128)} %get-tuple-element.23), channel_id=1, source_target_pairs={{1,0},{4,1},{5,4},{8,5},{9,8},{12,9},{13,12},{3,2},{6,3},{7,6},{10... | collective-permute-start | bytes 3538952 | tf_op jit(solution)/shard_map/ppermute | solution.py:462
  12.4 44.9 %collective-permute-start = (f32[72,4096]{1,0:T(8,128)}, f32[72,4096]{1,0:T(8,128)S(1)}, u32[]{:S(2)}, u32[]{:S(2)}) collective-permute-start(f32[72,4096]{1,0:T(8,128)} %get-tuple-element.22.own), channel_id=1, source_target_pairs={{0,1},{1,4},{4,5},{5,8},{8,9},{9,12},{12,13},{2,3},{3,6},{6,7},{7,... | collective-permute-start | bytes 3538952 | tf_op jit(solution)/shard_map/ppermute | solution.py:461
  57.3 1.0 %copy-start = (f32[72,4096]{1,0:T(8,128)}, f32[72,4096]{1,0:T(8,128)S(1)}, u32[]{:S(2)}) copy-start(f32[72,4096]{1,0:T(8,128)S(1)} %collective-permute-done.1.upper) | copy-start | bytes 3538948
  57.3 1.4 %copy-start.1 = (f32[72,4096]{1,0:T(8,128)}, f32[72,4096]{1,0:T(8,128)S(1)}, u32[]{:S(2)}) copy-start(f32[72,4096]{1,0:T(8,128)S(1)} %collective-permute-done.lower) | copy-start | bytes 3538948

commit v2 on v1

v2 whole, which is shorter than its diff:
```python
import functools

import jax
import jax.numpy as jnp
import numpy as np
from jax import lax
from jax.experimental import pallas as pl
from jax.experimental.pallas import tpu as pltpu
from jax.sharding import PartitionSpec as P

PTS = 256
RANK = 64
LEAVES = 32
NODES = 63
SLOTS = 8
REACH = 16
HALF = REACH * PTS
ROWS = 8
PAD = 16
GROUP = 4
WIDTH = 0.05
NEAR_WEIGHT = 0.0625
EMPTY = 3 * NODES
QUADS = 16
F32 = jnp.float32
BF16 = jnp.bfloat16
AXES = ("leaf", "sub")
NN = (((1,), (0,)), ((), ()))
NT = (((1,), (1,)), ((), ()))
TN = (((0,), (0,)), ((), ()))


def selections():
    source_part = (1, 1, 2, 2, 1, 3)
    target_part = (1, 2, 1, 2, 3, 1)
    source = np.zeros((64, 32), np.float32)
    target = np.zeros((32, 64), np.float32)
    for g in range(6):
        for c in range(3):
            source[(source_part[g] - 1) * 8 + c, 4 * g + c] = 1
            target[4 * g + c, (target_part[g] - 1) * 8 + c] = -2
        f = 4 * g + 3
        if g < 3:
            source[24 + 8 * g, f] = 1
            target[f, 48] = 1
        else:
            source[48, f] = 1
            target[f, 24 + 8 * (g - 3)] = 1
    source[48, 24] = 1
    target[24, 48] = 1
    return jnp.asarray(np.tile(source, (1, 4)), BF16), jnp.asarray(target, BF16)


def halves(x):
    high = x.astype(BF16)
    return high, (x - high.astype(F32)).astype(BF16)


def dot(a, b, dims=NN):
    return lax.dot_general(a, b, dims, preferred_element_type=F32)


def dot3(a, b, dims=NN):
    ah, al = halves(a)
    bh, bl = halves(b)
    rows = a.shape[0]
    both = dot(jnp.concatenate([ah, al], axis=0), bh, dims)
    return both[:rows] + both[rows:] + dot(ah, bl, dims)


def scaled(points):
    return (points - 0.5) * (1.0 / WIDTH)


def padded(points):
    return jnp.concatenate([points, jnp.zeros((5, points.shape[1]), F32)], axis=0)


def parts_of(c):
    n = c.shape[1]

    def rounded(x):
        return x.astype(BF16).astype(F32)

    p1 = rounded(c)
    rest = c - p1
    p2 = rounded(rest)
    p3 = rest - p2
    norm = jnp.broadcast_to(jnp.sum(c * c, axis=0, keepdims=True), (8, n))
    n1 = rounded(norm)
    rest = norm - n1
    n2 = rounded(rest)
    n3 = rest - n2
    rows = [p1, p2, p3, n1, n2, n3, jnp.ones((8, n), F32), jnp.zeros((8, n), F32)]
    return jnp.concatenate(rows, axis=0).astype(BF16)


def lower_lanes(rows):
    return lax.broadcasted_iota(jnp.int32, (rows, 128), 1) < RANK


def diagonal(x, vectors):
    return jnp.where(lower_lanes(vectors), x[:vectors], x[vectors:])


def spread_pair(pair):
    low = lower_lanes(pair.shape[0])
    zero = jnp.zeros_like(pair)
    return jnp.concatenate([jnp.where(low, pair, zero), jnp.where(low, zero, pair)], axis=0)


def pipelined(steps, first, second):
    for u in range(GROUP):
        first(u, u, 0)

    def body(i, carry):
        for h in range(2):
            base = (2 * i + h) * GROUP
            for u in range(GROUP):
                first(base + GROUP + u, u, 1 - h)
            for u in range(GROUP):
                second(base + u, u, h)
        return carry

    lax.fori_loop(0, (steps + 2 * GROUP - 1) // (2 * GROUP), body, 0)


class Copies:
    def __init__(self, sems):
        self.sems = sems
        self.count = 0

    def start(self, source, target):
        copy = pltpu.make_async_copy(source, target, self.sems.at[self.count])
        self.count += 1
        copy.start()
        return copy


def up_kernel(
    near_ref, far_ref, far_vec, charges_hbm, coords, basis_hbm, transfer_hbm,
    up_hbm, down_hbm, root_ref, local_ref, halo_ref, steps_ref, count_ref, entry_ref,
    charges, points, basis, transfer, coef, sems,
):
    vectors = charges.shape[0]
    start = Copies(sems).start
    quarter = LEAVES // 4
    in_charges, in_basis = [], []
    for i in range(4):
        lanes = slice(i * quarter * PTS, (i + 1) * quarter * PTS)
        leaves = slice(i * quarter, (i + 1) * quarter)
        in_charges.append(start(charges_hbm.at[:, lanes], charges.at[:, lanes]))
        in_basis.append(start(basis_hbm.at[leaves], basis.at[leaves]))
    in_transfer = start(transfer_hbm, transfer)
    device = lax.axis_index(AXES)
    first = device * LEAVES

    def scan_leaf(t, counts):
        here, there = counts
        for e in range(SLOTS):
            entry = near_ref[e, t]
            s = entry - first
            inside = jnp.logical_and(s >= 0, s < LEAVES)
            outside = jnp.logical_and(entry >= 0, jnp.logical_not(inside))
            local_ref[here] = t * 256 + s
            halo_ref[there] = t * 256 + jnp.where(s < 0, s + REACH, s - REACH)
            here = here + inside.astype(jnp.int32)
            there = there + outside.astype(jnp.int32)
        return here, there

    here, there = lax.fori_loop(0, LEAVES, scan_leaf, (jnp.int32(0), jnp.int32(0)))
    for u in range(PAD):
        local_ref[here + u] = LEAVES
        halo_ref[there + u] = LEAVES
    for q in range(QUADS):
        steps_ref[q] = q * 256 + 2 * q

    def scan_quad(q, count):
        top = far_ref[4, 4 * q]
        for e in range(4):
            for c in range(4):
                top = jnp.maximum(top, far_ref[4 + e, jnp.minimum(4 * q + c, NODES - 1)])
        steps_ref[count] = q * 256 + 2 * q + 1
        return count + (top >= 0).astype(jnp.int32)

    total = lax.fori_loop(0, QUADS, scan_quad, jnp.int32(QUADS))
    for u in range(PAD):
        steps_ref[total + u] = QUADS * 256
    count_ref[0] = here
    count_ref[1] = there
    count_ref[2] = total
    entry = far_vec[...]
    entry_ref[:, 0:NODES] = jnp.where(entry >= 0, entry - (device - 1) * NODES, EMPTY)
    entry_ref[:, NODES:64] = jnp.full((SLOTS, 1), EMPTY, jnp.int32)
    points[0:3] = coords[...]
    points[3:] = jnp.zeros((ROWS - 3, points.shape[1]), F32)

    out = [
        start(points.at[:, HALF:], up_hbm.at[2 * vectors :]),
        start(points.at[:, :HALF], down_hbm.at[2 * vectors :]),
    ]
    per = LEAVES // 8
    for p in range(LEAVES // 2):
        if p % per == 0:
            in_charges[p // per].wait()
            in_basis[p // per].wait()
            if p == per:
                out.append(start(charges.at[:, :HALF], down_hbm.at[0:vectors]))
            if p == 3 * per:
                out.append(start(charges.at[:, HALF:], up_hbm.at[0:vectors]))
        a, b = slice(2 * p * PTS, (2 * p + 1) * PTS), slice((2 * p + 1) * PTS, (2 * p + 2) * PTS)
        both = jnp.concatenate([charges[:, a], charges[:, b]], axis=0)
        value = diagonal(dot3(both, basis[2 * p : 2 * p + 2].reshape(2 * RANK, PTS), NT), vectors)
        coef[:, p * 128 : (p + 1) * 128] = value
    for hbm in (up_hbm, down_hbm):
        out.append(start(coef.at[:, :2048], hbm.at[vectors : 2 * vectors, :2048]))
    in_transfer.wait()
    for p in range(LEAVES // 2, LEAVES - 1):
        q = 2 * p - LEAVES
        both = jnp.concatenate(
            [coef[:, q * 128 : (q + 1) * 128], coef[:, (q + 1) * 128 : (q + 2) * 128]], axis=0
        )
        value = diagonal(dot3(both, transfer[q : q + 2].reshape(128, 128), NT), vectors)
        coef[:, p * 128 : (p + 1) * 128] = value
    root = dot3(coef[:, 30 * 128 : 31 * 128], transfer[30], NT)
    root = jnp.concatenate([root, jnp.zeros((vectors, RANK), F32)], axis=1)
    coef[:, 31 * 128 :] = root
    for hbm in (up_hbm, down_hbm):
        out.append(start(coef.at[:, 2048:], hbm.at[vectors : 2 * vectors, 2048:]))
    for g in range(root_ref.shape[0]):
        root_ref[g] = root
    for copy in out:
        copy.wait()


def source_tables(k, charges, points, select, sources, weights):
    parts = parts_of(points)
    sources[k] = dot(parts, select[:, 0:32], TN).astype(BF16)
    high, low = halves(charges)
    weights[k] = jnp.concatenate([high, low], axis=0)
    return parts


def near_steps(list_ref, sources, targets, weights, out_ref, tiles):
    vectors = out_ref.shape[0]
    highs = (tiles[:GROUP], tiles[GROUP : 2 * GROUP])
    lows = (tiles[2 * GROUP : 3 * GROUP], tiles[3 * GROUP :])

    def decode(j):
        code = list_ref[j]
        return lax.shift_right_logical(code, 8), jnp.bitwise_and(code, 255)

    def first(j, u, b):
        t, s = decode(j)
        high, low = halves(lax.rsqrt(dot(sources[s], targets[t])))
        highs[b][u][...] = high
        lows[b][u][...] = low

    def second(j, u, b):
        t, s = decode(j)
        q = weights[s]
        both = dot(q, highs[b][u][...])
        lanes = pl.ds(pl.multiple_of(t * PTS, PTS), PTS)
        out_ref[:, lanes] += both[:vectors] + both[vectors:] + dot(q[:vectors], lows[b][u][...])

    return first, second


def near_kernel(
    count_ref, list_ref, charges_hbm, coords, select, select_t,
    near_ref, targets_hbm,
    charges, targets, sources, weights, sems, *tiles,
):
    vectors = charges.shape[0]
    start = Copies(sems).start
    quarter = LEAVES // 4
    copies = []
    for i in range(4):
        lanes = slice(i * quarter * PTS, (i + 1) * quarter * PTS)
        copies.append(start(charges_hbm.at[:, lanes], charges.at[:, lanes]))
    near_ref[...] = jnp.zeros_like(near_ref)
    weights[LEAVES] = jnp.zeros((2 * vectors, PTS), BF16)
    for k in range(LEAVES):
        if k % quarter == 0:
            copies[k // quarter].wait()
        lanes = slice(k * PTS, (k + 1) * PTS)
        c = padded(scaled(coords[:, lanes]))
        parts = source_tables(k, charges[:, lanes], c, select, sources, weights)
        targets[k] = dot(select_t[...], parts).astype(BF16)
    sources[LEAVES] = sources[0]
    out = start(targets, targets_hbm)
    first, second = near_steps(list_ref, sources, targets, weights, near_ref, tiles)
    pipelined(count_ref[0], first, second)
    out.wait()


def down_kernel(
    groups, count_ref, list_ref, steps_ref, entry_ref,
    near_hbm, targets_hbm, lower_hbm, own_hbm, upper_hbm, basis_hbm, transfer_hbm,
    roots, skeleton, top_transfer, top_skeleton, select, select_t,
    out_hbm,
    near, targets, lower, own, upper, basis, transfer,
    sources, weights, nodes, pairs, feature, quads, coef_low, coef_high, local, top_coef,
    sems, *tiles,
):
    vectors = near.shape[0]
    device = lax.axis_index(AXES)
    low_mask = lower_lanes(vectors)
    coef_rows = slice(vectors, 2 * vectors)
    start = Copies(sems).start
    halo_in = []
    for hbm, vmem in ((lower_hbm, lower), (upper_hbm, upper)):
        halo_in.append(start(hbm.at[0:vectors], vmem.at[0:vectors]))
        halo_in.append(start(hbm.at[2 * vectors :], vmem.at[2 * vectors :]))
    near_in = [start(near_hbm, near), start(targets_hbm, targets)]
    coef_in = [
        start(hbm.at[coef_rows], vmem.at[coef_rows])
        for hbm, vmem in ((lower_hbm, lower), (own_hbm, own), (upper_hbm, upper))
    ]
    matrices_in = [start(transfer_hbm, transfer), start(basis_hbm, basis)]

    width = skeleton.shape[2]
    full = -(-width // 256) * 256
    raw = skeleton[...].reshape(3 * RANK, width)
    raw = jnp.concatenate([raw, jnp.zeros((3 * RANK, full - width), F32)], axis=1)
    shift = lax.rem(full - (device - 1) * NODES, full)
    window = pltpu.roll(raw, shift, 1)[:, :256]
    window = jnp.concatenate([scaled(window), jnp.zeros((RANK, 256), F32)], axis=0)
    window = window.T
    for i in range(2):
        nodes[i] = window[:, i * 128 : (i + 1) * 128]
    pairs[...] = jnp.zeros_like(pairs)
    for c in range(3):
        half = slice((c % 2) * RANK, (c % 2 + 1) * RANK)
        for base, first_node, count in ((0, 0, 96), (96, NODES, 32)):
            even = nodes[c // 2, pl.ds(first_node, count, stride=2), :][:, half]
            odd = nodes[c // 2, pl.ds(first_node + 1, count, stride=2), :][:, half]
            both = jnp.concatenate([even, odd], axis=1)
            pairs[pl.ds(base * 8 + c, count, stride=8), :] = both
    for g in range(24):
        c = jnp.concatenate([pairs[(4 * g + u) * 8 : (4 * g + u + 1) * 8] for u in range(4)], axis=1)
        value = dot(parts_of(c), select[...], TN).astype(BF16)
        feature[8 * g : 8 * g + 8] = value.reshape(8, RANK, 128)
    quad_lane = lax.broadcasted_iota(jnp.int32, (32, 256), 1) // RANK
    for q in range(QUADS):
        c = jnp.concatenate(
            [pairs[(96 + 2 * q + u) * 8 : (97 + 2 * q + u) * 8] for u in range(2)], axis=1
        )
        target = dot(select_t[...], parts_of(c))
        blocks = [jnp.where(quad_lane == i, target, 0.0) for i in range(4)]
        quads[q] = jnp.concatenate(blocks, axis=0).astype(BF16)

    for copy in halo_in:
        copy.wait()
    for k in range(LEAVES):
        buffer = lower if k < REACH else upper
        lanes = slice((k % REACH) * PTS, (k % REACH + 1) * PTS)
        c = padded(scaled(buffer[2 * vectors : 2 * vectors + 3, lanes]))
        source_tables(k, buffer[0:vectors, lanes], c, select, sources, weights)
    weights[LEAVES] = jnp.zeros((2 * vectors, PTS), BF16)
    sources[LEAVES] = sources[0]
    for copy in near_in:
        copy.wait()
    first, second = near_steps(list_ref, sources, targets, weights, near, tiles)
    pipelined(count_ref[1], first, second)

    for copy in coef_in:
        copy.wait()
    for b, buffer in enumerate((lower, own, upper)):
        for p in range(32):
            pair = buffer[coef_rows, p * 128 : (p + 1) * 128]
            swap = pltpu.roll(pair, RANK, 1)
            zero = jnp.zeros_like(pair)
            for n, (a, c) in enumerate(((pair, swap), (swap, pair))):
                if 2 * p + n == NODES:
                    continue
                for table, value in (
                    (coef_low, jnp.where(low_mask, a, zero)),
                    (coef_high, jnp.where(low_mask, zero, c)),
                ):
                    high, low = halves(value)
                    table[b * NODES + 2 * p + n] = jnp.concatenate([high, low], axis=0)
    coef_low[EMPTY] = jnp.zeros((2 * vectors, 128), BF16)
    coef_high[EMPTY] = jnp.zeros((2 * vectors, 128), BF16)
    local[...] = jnp.zeros_like(local)
    highs = (tiles[:GROUP], tiles[GROUP : 2 * GROUP])
    lows = (tiles[2 * GROUP : 3 * GROUP], tiles[3 * GROUP :])
    lane_group = lax.broadcasted_iota(jnp.int32, (RANK, 128), 1) // 32

    def entries(j):
        code = steps_ref[j]
        target = lax.shift_right_logical(code, 8)
        chunk = jnp.bitwise_and(code, 255)
        q = lax.shift_right_logical(chunk, 1)
        slot = 4 * jnp.bitwise_and(chunk, 1)
        return target, q, [[entry_ref[slot + e, 4 * q + i] for e in range(4)] for i in range(4)]

    def far_first(j, u, b):
        target, q, picks = entries(j)
        rows = []
        for e in range(4):
            value = feature[picks[3][e]]
            for i in range(3):
                value = jnp.where(lane_group == i, feature[picks[i][e]], value)
            rows.append(value)
        high, low = halves(lax.rsqrt(dot(jnp.concatenate(rows, axis=0), quads[q])))
        highs[b][u][...] = high
        lows[b][u][...] = low

    def far_second(j, u, b):
        target, q, picks = entries(j)
        sides = []
        for s in picks:
            left = coef_low[s[0]] + coef_high[s[1]]
            right = coef_low[s[2]] + coef_high[s[3]]
            sides.append(jnp.concatenate([left, right], axis=1))
        high = jnp.concatenate([side[:vectors] for side in sides], axis=0)
        low = jnp.concatenate([side[vectors:] for side in sides], axis=0)
        both = dot(jnp.concatenate([high, low], axis=0), highs[b][u][...])
        value = both[: 4 * vectors] + both[4 * vectors :] + dot(high, lows[b][u][...])
        local[2 * target] += diagonal(value[: 2 * vectors, :128], vectors)
        local[2 * target + 1] += diagonal(value[2 * vectors :, 128:], vectors)

    pipelined(count_ref[2], far_first, far_second)

    bits = groups.bit_length() - 1
    offsets = []
    offset = 0
    for h in range(bits):
        count = groups >> h
        offsets.append(offset)
        for i in range(count // 2):
            if h == 0:
                pair = roots[2 * i] + pltpu.roll(roots[2 * i + 1], RANK, 1)
            else:
                row = groups - (groups >> (h - 1)) + 2 * i
                below = offsets[h - 1] + 2 * i
                both = top_coef[below : below + 2].reshape(2 * vectors, 128)
                matrix = top_transfer[row : row + 2].reshape(128, 128)
                pair = diagonal(dot3(both, matrix, NT), vectors)
            top_coef[offset + i] = pair
        offset += count // 2
    upper_row = lax.broadcasted_iota(jnp.int32, (128, 128), 0) < RANK
    upper_lane = lax.broadcasted_iota(jnp.int32, (128, 128), 1) < RANK
    couple = []
    for h in range(bits):
        node = device // 2**h
        i = node // 2
        if h == 0:
            rows = [
                jnp.concatenate(
                    [nodes[c // 2, r : r + 1, c % 2 * RANK : (c % 2 + 1) * RANK] for c in range(3)],
                    axis=0,
                )
                for r in (NODES - 1, 2 * NODES - 1, 3 * NODES - 1)
            ]
            odd = node % 2 == 1
            left = jnp.where(odd, rows[0], rows[1])
            right = jnp.where(odd, rows[1], rows[2])
        else:
            row = groups - (groups >> (h - 1))
            left = scaled(top_skeleton[row + 2 * i])
            right = scaled(top_skeleton[row + 2 * i + 1])
        parts = parts_of(padded(jnp.concatenate([left, right], axis=1)))
        source = dot(parts, select[:, 0:32], TN).astype(BF16)
        target = dot(select_t[...], parts).astype(BF16)
        tile = jnp.where(upper_row != upper_lane, lax.rsqrt(dot(source, target)), 0.0)
        couple.append(dot3(top_coef[offsets[h] + i], tile))
    top = couple[bits - 1]
    for h in range(bits - 2, -1, -1):
        parent = device // 2 ** (h + 1)
        mine = jnp.where(low_mask == (parent % 2 == 0), top, 0.0)
        row = groups - (groups >> h) + 2 * (parent // 2)
        matrix = top_transfer[pl.ds(row, 2)].reshape(128, 128)
        top = couple[h] + dot3(mine, matrix)
    top = jnp.where(device % 2 == 1, pltpu.roll(top, RANK, 1), top)

    matrices_in[0].wait()
    local[30] += dot3(jnp.where(low_mask, local[31] + top, 0.0)[:, :RANK], transfer[30])
    for p in range(30, 15, -1):
        q = 2 * p - LEAVES
        both = dot3(spread_pair(local[p]), transfer[q : q + 2].reshape(128, 128))
        local[q] += both[:vectors]
        local[q + 1] += both[vectors:]
    matrices_in[1].wait()
    out = []
    for p in range(LEAVES // 2):
        both = dot3(spread_pair(local[p]), basis[2 * p : 2 * p + 2].reshape(128, PTS))
        for c in range(2):
            lanes = slice((2 * p + c) * PTS, (2 * p + c + 1) * PTS)
            near[:, lanes] = both[c * vectors : (c + 1) * vectors] + NEAR_WEIGHT * near[:, lanes]
        if p % 4 == 3:
            lanes = slice((p - 3) * 2 * PTS, (p + 1) * 2 * PTS)
            out.append(start(near.at[:, lanes], out_hbm.at[:, lanes]))
    for copy in out:
        copy.wait()


def whole(count, space=pltpu.VMEM):
    return [pl.BlockSpec(memory_space=space)] * count


def on_device(
    charges, coordinates, near_lists, far_lists, leaf_basis, local_transfer,
    skeleton, top_transfer, top_skeleton,
):
    vectors = charges.shape[0]
    groups = lax.axis_size(AXES)
    points = LEAVES * PTS
    height = 2 * vectors + ROWS
    shape = jax.ShapeDtypeStruct
    select, select_t = selections()
    params = pltpu.CompilerParams(vmem_limit_bytes=56 << 20)
    smem = pltpu.SMEM
    vmem = pltpu.VMEM
    matrices = [vmem((LEAVES, RANK, PTS), F32), vmem((LEAVES - 1, RANK, 128), F32)]
    up, down, root, local_list, halo_list, steps, counts, entries = pl.pallas_call(
        up_kernel,
        out_shape=[
            shape((height, HALF), F32),
            shape((height, HALF), F32),
            shape((groups, vectors, 128), F32),
            shape((LEAVES * SLOTS + PAD,), jnp.int32),
            shape((LEAVES * SLOTS + PAD,), jnp.int32),
            shape((2 * QUADS + PAD,), jnp.int32),
            shape((3,), jnp.int32),
            shape((SLOTS, 64), jnp.int32),
        ],
        in_specs=whole(2, smem) + whole(1) + whole(1, pl.ANY) + whole(1) + whole(2, pl.ANY),
        out_specs=whole(2, pl.ANY) + whole(1) + whole(4, smem) + whole(1),
        scratch_shapes=[vmem((vectors, points), F32), vmem((ROWS, points), F32)]
        + matrices
        + [vmem((vectors, 32 * 128), F32), pltpu.SemaphoreType.DMA((20,))],
        compiler_params=params,
    )(near_lists.T, far_lists.T, far_lists.T, charges, coordinates, leaf_basis, local_transfer)

    upward = [(i, i + 1) for i in range(groups - 1)]
    lower = lax.ppermute(up, AXES, upward)
    upper = lax.ppermute(down, AXES, [(j, i) for i, j in upward])
    roots = lax.all_to_all(root, AXES, 0, 0)

    tiles = [vmem((PTS, PTS), BF16)] * (4 * GROUP)
    tables = [vmem((LEAVES + 1, PTS, 32), BF16), vmem((LEAVES + 1, 2 * vectors, PTS), BF16)]
    near, targets = pl.pallas_call(
        near_kernel,
        out_shape=[shape((vectors, points), F32), shape((LEAVES, 32, PTS), BF16)],
        in_specs=whole(2, smem) + whole(1, pl.ANY) + whole(3),
        out_specs=whole(1) + whole(1, pl.ANY),
        scratch_shapes=[vmem((vectors, points), F32), vmem((LEAVES, 32, PTS), BF16)]
        + tables
        + [pltpu.SemaphoreType.DMA((5,))]
        + tiles,
        compiler_params=params,
        cost_estimate=pl.CostEstimate(
            flops=192 * 3 * 2 * PTS**3, transcendentals=192 * PTS**2, bytes_accessed=4 << 20
        ),
    )(counts, local_list, charges, coordinates, select, select_t)

    return pl.pallas_call(
        functools.partial(down_kernel, groups),
        out_shape=shape((vectors, points), F32),
        in_specs=whole(4, smem) + whole(7, pl.ANY) + whole(6),
        out_specs=pl.BlockSpec(memory_space=pl.ANY),
        scratch_shapes=[vmem((vectors, points), F32), vmem((LEAVES, 32, PTS), BF16)]
        + [vmem((height, HALF), F32)] * 3
        + matrices
        + tables
        + [
            vmem((2, 256, 128), F32),
            vmem((128 * 8, 128), F32),
            vmem((192, RANK, 128), BF16),
            vmem((QUADS, 128, 256), BF16),
            vmem((EMPTY + 1, 2 * vectors, 128), BF16),
            vmem((EMPTY + 1, 2 * vectors, 128), BF16),
            vmem((2 * QUADS + 2, vectors, 128), F32),
            vmem((groups, vectors, 128), F32),
            pltpu.SemaphoreType.DMA((16,)),
        ]
        + tiles,
        compiler_params=params,
    )(
        counts, halo_list, steps, entries, near, targets, lower, up, upper,
        leaf_basis, local_transfer, roots, skeleton.transpose(1, 2, 0),
        top_transfer, top_skeleton, select, select_t,
    )


def solution(mesh):
    placed = (
        P("vec", ("parts", "leaf", "sub")),
        P(None, ("parts", "leaf", "sub")),
        P(("parts", "leaf", "sub"), None),
        P(("parts", "leaf", "sub"), None),
        P(("parts", "leaf", "sub"), None, None),
        P(("parts", "leaf", "sub"), None, None),
        P("parts", None, None),
        P("parts", None, None),
        P("parts", None, None),
    )
    return jax.shard_map(
        on_device,
        mesh=mesh,
        in_specs=placed,
        out_specs=P("vec", ("parts", "leaf", "sub")),
        check_vma=False,
    )
```

time: 82.4 us -> 58.4 us (0.71)
  blocking collectives: 22.6 us -> 0 us
  starting transfers between devices: 6.51 us -> 11.9 us
  local copies, waits for them, and re-layouts: 5.49 us -> 1.42 us
  Pallas kernels: 47.7 us -> 45 us
    all_gather x1 -> x0, blocking collectives: 22.6 us -> none  [on_device(): roots = lax.all_gather(root, AXES)]
    all_to_all x0 -> x1, starting transfers between devices: none -> 6.39 us  [on_device(): roots = lax.all_to_all(root, AXES, 0, 0)]
    pallas_call x1, Pallas kernels: 23.6 us -> 18 us  [on_device(): pl.pallas_call(functools.partial(down_kernel, groups), out_shape=shape((v...]
    unnamed x11 -> x6, local copies, waits for them, and re-layouts: 5.49 us -> 1.42 us
    pallas_call x1, Pallas kernels: 16.4 us -> 19.6 us  [on_device(): pl.pallas_call(near_kernel, out_shape=[shape((vectors, points), F32), sha...]
    ppermute x1, starting transfers between devices: 4.55 us -> 3.64 us  [on_device(): lower = lax.ppermute(up, AXES, upward)]
  transfers between devices with their start and end apart: 2 -> 3, of which waited for: 0 -> 0; matrix products, arithmetic and copies ran while one was open for 2% -> 0% of each run, Pallas kernels for 20% -> 33%
where the time goes in v2:
time: 58.4 us; the launch traced here: 58.5 us
  Pallas kernels  45 us (77%)
  starting transfers between devices  11.9 us (20%)
  local copies, waits for them, and re-layouts  1.42 us (2%)
    pallas_call x1, Pallas kernels, on_device(): pl.pallas_call(near_kernel, out_shape=[shape((vectors, points), F32), sha...  19.6 us
    pallas_call x1, Pallas kernels, on_device(): pl.pallas_call(functools.partial(down_kernel, groups), out_shape=shape((v...  18 us
    pallas_call x1, Pallas kernels, on_device(): pl.pallas_call(up_kernel, out_shape=[shape((height, HALF), F32), shape((h...  7.41 us
    all_to_all x1, starting transfers between devices, on_device(): roots = lax.all_to_all(root, AXES, 0, 0)  6.39 us
    ppermute x1, starting transfers between devices, on_device(): lower = lax.ppermute(up, AXES, upward)  3.64 us
    ppermute x1, starting transfers between devices, on_device(): upper = lax.ppermute(down, AXES, [(j, i) for i, j in upward])  1.91 us
    unnamed x6, local copies, waits for them, and re-layouts  1.42 us
  transfers between devices with their start and end apart: 3, of which 0 were waited for; matrix products, arithmetic and copies ran while one was open for 0% of the time, Pallas kernels for 33%

profile of v2, /device:TPU:1, one launch (start us, length us, event | category | flops | bytes accessed | tf_op | source)
XLA Modules:
  0.0 58.5 jit_solution(10357335275811797646)
XLA Ops:
  0.0 7.4 %shard_map.109 = (f32[72,4096]{1,0:T(8,128)}, f32[72,4096]{1,0:T(8,128)}, f32[8,32,128]{2,1,0:T(8,128)}, s32[272]{0:T(512)}, s32[272]{0:T(512)}, /*index=5*/s32[48]{0:T(128)}, s32[3]{0:T(128)}, s32[8,64]{1,0:T(8,128)}) custom-call(s32[8,32]{1,0:T(8,128)} %bitcast.6, s32[8,63]{1,0:T(8,128)} %bitcast.4, s32[8,63]{1,0:T(8,128)} %bitcast.5, ...), custom_call_target="tpu_custom_call" | custom-call | tf_op jit(solution)/shard_map/pallas_call | solution.py:517
  7.4 6.4 %all-to-all-start = ((f32[8,32,128]{2,1,0:T(8,128)}), f32[8,32,128]{2,1,0:T(8,128)S(1)}, u32[]{:S(2)}, u32[]{:S(2)}) async-start(f32[8,32,128]{2,1,0:T(8,128)} %get-tuple-element.24), calls=%async_computation | async-start | bytes 262144 | tf_op jit(solution)/shard_map/all_to_all | solution.py:540
  13.8 1.9 %collective-permute-start.1 = (f32[72,4096]{1,0:T(8,128)}, f32[72,4096]{1,0:T(8,128)S(1)}, u32[]{:S(2)}, u32[]{:S(2)}) collective-permute-start(f32[72,4096]{1,0:T(8,128)} %get-tuple-element.23), channel_id=1, source_target_pairs={{1,0},{4,1},{5,4},{8,5},{9,8},{12,9},{13,12},{3,2},{6,3},{7,6},{10... | collective-permute-start | bytes 3538952 | tf_op jit(solution)/shard_map/ppermute | solution.py:539
  15.7 3.6 %collective-permute-start = (f32[72,4096]{1,0:T(8,128)}, f32[72,4096]{1,0:T(8,128)S(1)}, u32[]{:S(2)}, u32[]{:S(2)}) collective-permute-start(f32[72,4096]{1,0:T(8,128)} %get-tuple-element.22.own_hbm), channel_id=1, source_target_pairs={{0,1},{1,4},{4,5},{5,8},{8,9},{9,12},{12,13},{2,3},{3,6},{6,7},{7,... | collective-permute-start | bytes 3538952 | tf_op jit(solution)/shard_map/ppermute | solution.py:538
  19.4 19.6 %shard_map.110 = (f32[32,8192]{1,0:T(8,128)}, bf16[32,32,256]{2,1,0:T(8,128)(2,1)}) custom-call(s32[3]{0:T(128)} %get-tuple-element.15.count_ref, s32[272]{0:T(512)} %get-tuple-element.19.list_ref, f32[32,8192]{1,0:T(8,128)} %charges_hbm.3, f32[3,8192]{1,0:T(4,128)} %coords.3, bf16[64,128]{1,0:T(8,128)(2,1)} %constant.4.clone.select, ...), custom_call_target="tpu_custom_call" | custom-call | flops 19327352832 | bytes 4194304 | tf_op jit(solution)/shard_map/pallas_call | solution.py:544
  39.0 0.0 all-to-all-done.roots
  39.0 0.0 copy-start.2
  39.0 0.0 collective-permute-done.1.upper_hbm
  39.0 0.0 copy-start
  39.0 0.0 collective-permute-done.lower_hbm
  39.0 0.0 copy-start.1
  39.0 0.6 %copy-done.2 = f32[8,32,128]{2,1,0:T(8,128)} copy-done((f32[8,32,128]{2,1,0:T(8,128)}, f32[8,32,128]{2,1,0:T(8,128)S(1)}, u32[]{:S(2)}) %copy-start.2) | copy-done | bytes 131096
  39.6 0.4 copy-done
  40.0 0.4 copy-done.1
  40.4 18.0 %shard_map.111 = f32[32,8192]{1,0:T(8,128)} custom-call(s32[3]{0:T(128)} %get-tuple-element.15.count_ref, s32[272]{0:T(512)} %get-tuple-element.16.list_ref, s32[48]{0:T(128)} %get-tuple-element.17.steps_ref, s32[8,64]{1,0:T(8,128)} %get-tuple-element.18.entry_ref, f32[32,8192]{1,0:T(8,128)} %get-tuple-element.20.near_hbm, ...), custom_call_target="tpu_custom_call" | custom-call | tf_op jit(solution)/shard_map/pallas_call | solution.py:559
Async XLA Ops:
  7.4 31.5 %all-to-all-start = ((f32[8,32,128]{2,1,0:T(8,128)}), f32[8,32,128]{2,1,0:T(8,128)S(1)}, u32[]{:S(2)}, u32[]{:S(2)}) async-start(f32[8,32,128]{2,1,0:T(8,128)} %get-tuple-element.24), calls=%async_computation | async-start | bytes 262144 | tf_op jit(solution)/shard_map/all_to_all | solution.py:540
  13.8 25.2 %collective-permute-start.1 = (f32[72,4096]{1,0:T(8,128)}, f32[72,4096]{1,0:T(8,128)S(1)}, u32[]{:S(2)}, u32[]{:S(2)}) collective-permute-start(f32[72,4096]{1,0:T(8,128)} %get-tuple-element.23), channel_id=1, source_target_pairs={{1,0},{4,1},{5,4},{8,5},{9,8},{12,9},{13,12},{3,2},{6,3},{7,6},{10... | collective-permute-start | bytes 3538952 | tf_op jit(solution)/shard_map/ppermute | solution.py:539
  15.7 23.3 %collective-permute-start = (f32[72,4096]{1,0:T(8,128)}, f32[72,4096]{1,0:T(8,128)S(1)}, u32[]{:S(2)}, u32[]{:S(2)}) collective-permute-start(f32[72,4096]{1,0:T(8,128)} %get-tuple-element.22.own_hbm), channel_id=1, source_target_pairs={{0,1},{1,4},{4,5},{5,8},{8,9},{9,12},{12,13},{2,3},{3,6},{6,7},{7,... | collective-permute-start | bytes 3538952 | tf_op jit(solution)/shard_map/ppermute | solution.py:538
  39.0 0.6 %copy-start.2 = (f32[8,32,128]{2,1,0:T(8,128)}, f32[8,32,128]{2,1,0:T(8,128)S(1)}, u32[]{:S(2)}) copy-start(f32[8,32,128]{2,1,0:T(8,128)S(1)} %all-to-all-done.roots) | copy-start | bytes 393220
  39.0 1.0 %copy-start = (f32[72,4096]{1,0:T(8,128)}, f32[72,4096]{1,0:T(8,128)S(1)}, u32[]{:S(2)}) copy-start(f32[72,4096]{1,0:T(8,128)S(1)} %collective-permute-done.1.upper_hbm) | copy-start | bytes 3538948
  39.0 1.4 %copy-start.1 = (f32[72,4096]{1,0:T(8,128)}, f32[72,4096]{1,0:T(8,128)S(1)}, u32[]{:S(2)}) copy-start(f32[72,4096]{1,0:T(8,128)S(1)} %collective-permute-done.lower_hbm) | copy-start | bytes 3538948

commit v3 on v2

--- a/solution.py
+++ b/solution.py
@@ -17,6 +17,11 @@
 HALF = REACH * PTS
 ROWS = 8
 PAD = 16
+HALO = LEAVES * SLOTS + PAD
+STEPS = 2 * HALO
+COUNTS = STEPS + 48
+LISTS = COUNTS + 16
+LOCAL_GROUP = 6
 GROUP = 4
 WIDTH = 0.05
 NEAR_WEIGHT = 0.0625
@@ -109,20 +114,37 @@
     return jnp.concatenate([jnp.where(low, pair, zero), jnp.where(low, zero, pair)], axis=0)
 
 
-def pipelined(steps, first, second):
-    for u in range(GROUP):
+def pipelined(steps, group, first, second):
+    def both(base, h):
+        for u in range(group):
+            first(base + group + u, u, 1 - h)
+        for u in range(group):
+            second(base + u, u, h)
+
+    def last(base, h):
+        for u in range(group):
+            second(base + u, u, h)
+
+    for u in range(group):
         first(u, u, 0)
+    more = jnp.maximum((steps + group - 1) // group, 1) - 1
 
     def body(i, carry):
-        for h in range(2):
-            base = (2 * i + h) * GROUP
-            for u in range(GROUP):
-                first(base + GROUP + u, u, 1 - h)
-            for u in range(GROUP):
-                second(base + u, u, h)
+        both(2 * i * group, 0)
+        both((2 * i + 1) * group, 1)
         return carry
 
-    lax.fori_loop(0, (steps + 2 * GROUP - 1) // (2 * GROUP), body, 0)
+    lax.fori_loop(0, more // 2, body, 0)
+    base = more // 2 * 2 * group
+
+    @pl.when(more % 2 == 1)
+    def _():
+        both(base, 0)
+        last(base + group, 1)
+
+    @pl.when(more % 2 == 0)
+    def _():
+        last(base, 0)
 
 
 class Copies:
@@ -138,22 +160,31 @@
 
 
 def up_kernel(
-    near_ref, far_ref, far_vec, charges_hbm, coords, basis_hbm, transfer_hbm,
-    up_hbm, down_hbm, root_ref, local_ref, halo_ref, steps_ref, count_ref, entry_ref,
+    near_hbm, far_hbm, charges_hbm, coords_hbm, basis_hbm, transfer_hbm,
+    up_hbm, down_hbm, root_hbm, list_hbm, entry_hbm,
+    near_ref, far_ref, far_vec, coords, root_ref, list_ref, entry_ref,
     charges, points, basis, transfer, coef, sems,
 ):
     vectors = charges.shape[0]
     start = Copies(sems).start
     quarter = LEAVES // 4
-    in_charges, in_basis = [], []
-    for i in range(4):
+    in_lists = [start(near_hbm, near_ref), start(far_hbm, far_ref)]
+    in_vectors = [start(far_hbm, far_vec), start(coords_hbm, coords)]
+    incoming = []
+
+    def fetch(i):
         lanes = slice(i * quarter * PTS, (i + 1) * quarter * PTS)
         leaves = slice(i * quarter, (i + 1) * quarter)
-        in_charges.append(start(charges_hbm.at[:, lanes], charges.at[:, lanes]))
-        in_basis.append(start(basis_hbm.at[leaves], basis.at[leaves]))
+        incoming.append(start(charges_hbm.at[:, lanes], charges.at[:, lanes]))
+        incoming.append(start(basis_hbm.at[leaves], basis.at[leaves]))
+
+    for i in range(4):
+        fetch(i)
     in_transfer = start(transfer_hbm, transfer)
     device = lax.axis_index(AXES)
     first = device * LEAVES
+    for copy in in_lists:
+        copy.wait()
 
     def scan_leaf(t, counts):
         here, there = counts
@@ -162,33 +193,35 @@
             s = entry - first
             inside = jnp.logical_and(s >= 0, s < LEAVES)
             outside = jnp.logical_and(entry >= 0, jnp.logical_not(inside))
-            local_ref[here] = t * 256 + s
-            halo_ref[there] = t * 256 + jnp.where(s < 0, s + REACH, s - REACH)
+            list_ref[here] = t * 256 + s
+            list_ref[there] = t * 256 + jnp.where(s < 0, s + REACH, s - REACH)
             here = here + inside.astype(jnp.int32)
             there = there + outside.astype(jnp.int32)
         return here, there
 
-    here, there = lax.fori_loop(0, LEAVES, scan_leaf, (jnp.int32(0), jnp.int32(0)))
+    here, there = lax.fori_loop(0, LEAVES, scan_leaf, (jnp.int32(0), jnp.int32(HALO)))
     for u in range(PAD):
-        local_ref[here + u] = LEAVES
-        halo_ref[there + u] = LEAVES
+        list_ref[here + u] = LEAVES
+        list_ref[there + u] = LEAVES
     for q in range(QUADS):
-        steps_ref[q] = q * 256 + 2 * q
+        list_ref[STEPS + q] = q * 256 + 2 * q
 
     def scan_quad(q, count):
         top = far_ref[4, 4 * q]
         for e in range(4):
             for c in range(4):
                 top = jnp.maximum(top, far_ref[4 + e, jnp.minimum(4 * q + c, NODES - 1)])
-        steps_ref[count] = q * 256 + 2 * q + 1
+        list_ref[count] = q * 256 + 2 * q + 1
         return count + (top >= 0).astype(jnp.int32)
 
-    total = lax.fori_loop(0, QUADS, scan_quad, jnp.int32(QUADS))
+    total = lax.fori_loop(0, QUADS, scan_quad, jnp.int32(STEPS + QUADS))
     for u in range(PAD):
-        steps_ref[total + u] = QUADS * 256
-    count_ref[0] = here
-    count_ref[1] = there
-    count_ref[2] = total
+        list_ref[total + u] = QUADS * 256
+    list_ref[COUNTS] = here
+    list_ref[COUNTS + 1] = there - HALO
+    list_ref[COUNTS + 2] = total - STEPS
+    for copy in in_vectors:
+        copy.wait()
     entry = far_vec[...]
     entry_ref[:, 0:NODES] = jnp.where(entry >= 0, entry - (device - 1) * NODES, EMPTY)
     entry_ref[:, NODES:64] = jnp.full((SLOTS, 1), EMPTY, jnp.int32)
@@ -196,14 +229,17 @@
     points[3:] = jnp.zeros((ROWS - 3, points.shape[1]), F32)
 
     out = [
+        start(list_ref, list_hbm),
+        start(entry_ref, entry_hbm),
         start(points.at[:, HALF:], up_hbm.at[2 * vectors :]),
         start(points.at[:, :HALF], down_hbm.at[2 * vectors :]),
     ]
     per = LEAVES // 8
     for p in range(LEAVES // 2):
         if p % per == 0:
-            in_charges[p // per].wait()
-            in_basis[p // per].wait()
+            i = p // per
+            incoming[2 * i].wait()
+            incoming[2 * i + 1].wait()
             if p == per:
                 out.append(start(charges.at[:, :HALF], down_hbm.at[0:vectors]))
             if p == 3 * per:
@@ -229,6 +265,7 @@
         out.append(start(coef.at[:, 2048:], hbm.at[vectors : 2 * vectors, 2048:]))
     for g in range(root_ref.shape[0]):
         root_ref[g] = root
+    out.append(start(root_ref, root_hbm))
     for copy in out:
         copy.wait()
 
@@ -241,13 +278,17 @@
     return parts
 
 
-def near_steps(list_ref, sources, targets, weights, out_ref, tiles):
+def empty_source(sources, weights):
+    weights[LEAVES] = jnp.zeros(weights.shape[1:], BF16)
+    sources[LEAVES] = sources[0]
+
+
+def near_steps(list_ref, base, targets, tables, out_ref, highs, lows):
+    sources, weights = tables
     vectors = out_ref.shape[0]
-    highs = (tiles[:GROUP], tiles[GROUP : 2 * GROUP])
-    lows = (tiles[2 * GROUP : 3 * GROUP], tiles[3 * GROUP :])
 
     def decode(j):
-        code = list_ref[j]
+        code = list_ref[base + j]
         return lax.shift_right_logical(code, 8), jnp.bitwise_and(code, 255)
 
     def first(j, u, b):
@@ -267,57 +308,78 @@
 
 
 def near_kernel(
-    count_ref, list_ref, charges_hbm, coords, select, select_t,
-    near_ref, targets_hbm,
-    charges, targets, sources, weights, sems, *tiles,
+    list_hbm, charges_hbm, coords_hbm, select_hbm, select_t_hbm,
+    near_hbm, targets_hbm,
+    list_ref, coords, select, select_t, near_ref,
+    charges, targets, *rest,
 ):
-    vectors = charges.shape[0]
+    tables, sems, tiles = rest[:2], rest[2], rest[3:]
+    highs = (tiles[:LOCAL_GROUP], tiles[LOCAL_GROUP : 2 * LOCAL_GROUP])
+    lows = (tiles[2 * LOCAL_GROUP : 3 * LOCAL_GROUP], tiles[3 * LOCAL_GROUP :])
     start = Copies(sems).start
     quarter = LEAVES // 4
+    small = [start(coords_hbm, coords), start(select_hbm, select), start(select_t_hbm, select_t)]
     copies = []
     for i in range(4):
         lanes = slice(i * quarter * PTS, (i + 1) * quarter * PTS)
         copies.append(start(charges_hbm.at[:, lanes], charges.at[:, lanes]))
+    in_list = start(list_hbm, list_ref)
     near_ref[...] = jnp.zeros_like(near_ref)
-    weights[LEAVES] = jnp.zeros((2 * vectors, PTS), BF16)
+    for copy in small:
+        copy.wait()
     for k in range(LEAVES):
         if k % quarter == 0:
             copies[k // quarter].wait()
         lanes = slice(k * PTS, (k + 1) * PTS)
         c = padded(scaled(coords[:, lanes]))
-        parts = source_tables(k, charges[:, lanes], c, select, sources, weights)
+        parts = source_tables(k, charges[:, lanes], c, select, *tables)
         targets[k] = dot(select_t[...], parts).astype(BF16)
-    sources[LEAVES] = sources[0]
+    empty_source(*tables)
     out = start(targets, targets_hbm)
-    first, second = near_steps(list_ref, sources, targets, weights, near_ref, tiles)
-    pipelined(count_ref[0], first, second)
+    in_list.wait()
+    first, second = near_steps(list_ref, 0, targets, tables, near_ref, highs, lows)
+    pipelined(list_ref[COUNTS], LOCAL_GROUP, first, second)
+    out_near = start(near_ref, near_hbm)
     out.wait()
+    out_near.wait()
 
 
 def down_kernel(
-    groups, count_ref, list_ref, steps_ref, entry_ref,
+    groups, list_hbm, entry_hbm,
     near_hbm, targets_hbm, lower_hbm, own_hbm, upper_hbm, basis_hbm, transfer_hbm,
-    roots, skeleton, top_transfer, top_skeleton, select, select_t,
+    roots_hbm, skeleton_hbm, top_transfer_hbm, top_skeleton_hbm, select_hbm, select_t_hbm,
     out_hbm,
-    near, targets, lower, own, upper, basis, transfer,
-    sources, weights, nodes, pairs, feature, quads, coef_low, coef_high, local, top_coef,
+    list_ref, entry_ref, roots, skeleton, top_transfer, top_skeleton, select, select_t,
+    near, near_local, targets, lower, own, upper, basis, transfer,
+    sources, weights,
+    nodes, pairs, feature, quads, coef_low, coef_high, local, top_coef,
     sems, *tiles,
 ):
+    tables = (sources, weights)
+    highs = (tiles[:GROUP], tiles[GROUP : 2 * GROUP])
+    lows = (tiles[2 * GROUP : 3 * GROUP], tiles[3 * GROUP :])
     vectors = near.shape[0]
     device = lax.axis_index(AXES)
     low_mask = lower_lanes(vectors)
     coef_rows = slice(vectors, 2 * vectors)
     start = Copies(sems).start
-    halo_in = []
+    skeleton_in = [
+        start(skeleton_hbm, skeleton),
+        start(select_hbm, select),
+        start(select_t_hbm, select_t),
+    ]
+    for copy in skeleton_in:
+        copy.wait()
+    halo_in = [
+        start(roots_hbm, roots),
+        start(top_transfer_hbm, top_transfer),
+        start(top_skeleton_hbm, top_skeleton),
+        start(list_hbm, list_ref),
+        start(entry_hbm, entry_ref),
+    ]
     for hbm, vmem in ((lower_hbm, lower), (upper_hbm, upper)):
         halo_in.append(start(hbm.at[0:vectors], vmem.at[0:vectors]))
         halo_in.append(start(hbm.at[2 * vectors :], vmem.at[2 * vectors :]))
-    near_in = [start(near_hbm, near), start(targets_hbm, targets)]
-    coef_in = [
-        start(hbm.at[coef_rows], vmem.at[coef_rows])
-        for hbm, vmem in ((lower_hbm, lower), (own_hbm, own), (upper_hbm, upper))
-    ]
-    matrices_in = [start(transfer_hbm, transfer), start(basis_hbm, basis)]
 
     width = skeleton.shape[2]
     full = -(-width // 256) * 256
@@ -352,77 +414,9 @@
 
     for copy in halo_in:
         copy.wait()
-    for k in range(LEAVES):
-        buffer = lower if k < REACH else upper
-        lanes = slice((k % REACH) * PTS, (k % REACH + 1) * PTS)
-        c = padded(scaled(buffer[2 * vectors : 2 * vectors + 3, lanes]))
-        source_tables(k, buffer[0:vectors, lanes], c, select, sources, weights)
-    weights[LEAVES] = jnp.zeros((2 * vectors, PTS), BF16)
-    sources[LEAVES] = sources[0]
-    for copy in near_in:
-        copy.wait()
-    first, second = near_steps(list_ref, sources, targets, weights, near, tiles)
-    pipelined(count_ref[1], first, second)
-
-    for copy in coef_in:
-        copy.wait()
-    for b, buffer in enumerate((lower, own, upper)):
-        for p in range(32):
-            pair = buffer[coef_rows, p * 128 : (p + 1) * 128]
-            swap = pltpu.roll(pair, RANK, 1)
-            zero = jnp.zeros_like(pair)
-            for n, (a, c) in enumerate(((pair, swap), (swap, pair))):
-                if 2 * p + n == NODES:
-                    continue
-                for table, value in (
-                    (coef_low, jnp.where(low_mask, a, zero)),
-                    (coef_high, jnp.where(low_mask, zero, c)),
-                ):
-                    high, low = halves(value)
-                    table[b * NODES + 2 * p + n] = jnp.concatenate([high, low], axis=0)
-    coef_low[EMPTY] = jnp.zeros((2 * vectors, 128), BF16)
-    coef_high[EMPTY] = jnp.zeros((2 * vectors, 128), BF16)
-    local[...] = jnp.zeros_like(local)
-    highs = (tiles[:GROUP], tiles[GROUP : 2 * GROUP])
-    lows = (tiles[2 * GROUP : 3 * GROUP], tiles[3 * GROUP :])
-    lane_group = lax.broadcasted_iota(jnp.int32, (RANK, 128), 1) // 32
-
-    def entries(j):
-        code = steps_ref[j]
-        target = lax.shift_right_logical(code, 8)
-        chunk = jnp.bitwise_and(code, 255)
-        q = lax.shift_right_logical(chunk, 1)
-        slot = 4 * jnp.bitwise_and(chunk, 1)
-        return target, q, [[entry_ref[slot + e, 4 * q + i] for e in range(4)] for i in range(4)]
-
-    def far_first(j, u, b):
-        target, q, picks = entries(j)
-        rows = []
-        for e in range(4):
-            value = feature[picks[3][e]]
-            for i in range(3):
-                value = jnp.where(lane_group == i, feature[picks[i][e]], value)
-            rows.append(value)
-        high, low = halves(lax.rsqrt(dot(jnp.concatenate(rows, axis=0), quads[q])))
-        highs[b][u][...] = high
-        lows[b][u][...] = low
-
-    def far_second(j, u, b):
-        target, q, picks = entries(j)
-        sides = []
-        for s in picks:
-            left = coef_low[s[0]] + coef_high[s[1]]
-            right = coef_low[s[2]] + coef_high[s[3]]
-            sides.append(jnp.concatenate([left, right], axis=1))
-        high = jnp.concatenate([side[:vectors] for side in sides], axis=0)
-        low = jnp.concatenate([side[vectors:] for side in sides], axis=0)
-        both = dot(jnp.concatenate([high, low], axis=0), highs[b][u][...])
-        value = both[: 4 * vectors] + both[4 * vectors :] + dot(high, lows[b][u][...])
-        local[2 * target] += diagonal(value[: 2 * vectors, :128], vectors)
-        local[2 * target + 1] += diagonal(value[2 * vectors :, 128:], vectors)
-
-    pipelined(count_ref[2], far_first, far_second)
-
+    coef_in = [start(targets_hbm, targets)]
+    for hbm, vmem in ((lower_hbm, lower), (own_hbm, own), (upper_hbm, upper)):
+        coef_in.append(start(hbm.at[coef_rows], vmem.at[coef_rows]))
     bits = groups.bit_length() - 1
     offsets = []
     offset = 0
@@ -475,20 +469,88 @@
         top = couple[h] + dot3(mine, matrix)
     top = jnp.where(device % 2 == 1, pltpu.roll(top, RANK, 1), top)
 
-    matrices_in[0].wait()
+    for k in range(LEAVES):
+        buffer = lower if k < REACH else upper
+        lanes = slice((k % REACH) * PTS, (k % REACH + 1) * PTS)
+        c = padded(scaled(buffer[2 * vectors : 2 * vectors + 3, lanes]))
+        source_tables(k, buffer[0:vectors, lanes], c, select, *tables)
+    empty_source(*tables)
+    for copy in coef_in:
+        copy.wait()
+    late_in = [start(transfer_hbm, transfer), start(basis_hbm, basis), start(near_hbm, near_local)]
+    near[...] = jnp.zeros_like(near)
+    for b, buffer in enumerate((lower, own, upper)):
+        for p in range(32):
+            pair = buffer[coef_rows, p * 128 : (p + 1) * 128]
+            swap = pltpu.roll(pair, RANK, 1)
+            zero = jnp.zeros_like(pair)
+            for n, (a, c) in enumerate(((pair, swap), (swap, pair))):
+                if 2 * p + n == NODES:
+                    continue
+                for table, value in (
+                    (coef_low, jnp.where(low_mask, a, zero)),
+                    (coef_high, jnp.where(low_mask, zero, c)),
+                ):
+                    high, low = halves(value)
+                    table[b * NODES + 2 * p + n] = jnp.concatenate([high, low], axis=0)
+    coef_low[EMPTY] = jnp.zeros((2 * vectors, 128), BF16)
+    coef_high[EMPTY] = jnp.zeros((2 * vectors, 128), BF16)
+    local[...] = jnp.zeros_like(local)
+    lane_group = lax.broadcasted_iota(jnp.int32, (RANK, 128), 1) // 32
+
+    def entries(j):
+        code = list_ref[STEPS + j]
+        target = lax.shift_right_logical(code, 8)
+        chunk = jnp.bitwise_and(code, 255)
+        q = lax.shift_right_logical(chunk, 1)
+        slot = 4 * jnp.bitwise_and(chunk, 1)
+        return target, q, [[entry_ref[slot + e, 4 * q + i] for e in range(4)] for i in range(4)]
+
+    def far_first(j, u, b):
+        target, q, picks = entries(j)
+        rows = []
+        for e in range(4):
+            value = feature[picks[3][e]]
+            for i in range(3):
+                value = jnp.where(lane_group == i, feature[picks[i][e]], value)
+            rows.append(value)
+        high, low = halves(lax.rsqrt(dot(jnp.concatenate(rows, axis=0), quads[q])))
+        highs[b][u][...] = high
+        lows[b][u][...] = low
+
+    def far_second(j, u, b):
+        target, q, picks = entries(j)
+        sides = []
+        for s in picks:
+            left = coef_low[s[0]] + coef_high[s[1]]
+            right = coef_low[s[2]] + coef_high[s[3]]
+            sides.append(jnp.concatenate([left, right], axis=1))
+        high = jnp.concatenate([side[:vectors] for side in sides], axis=0)
+        low = jnp.concatenate([side[vectors:] for side in sides], axis=0)
+        both = dot(jnp.concatenate([high, low], axis=0), highs[b][u][...])
+        value = both[: 4 * vectors] + both[4 * vectors :] + dot(high, lows[b][u][...])
+        local[2 * target] += diagonal(value[: 2 * vectors, :128], vectors)
+        local[2 * target + 1] += diagonal(value[2 * vectors :, 128:], vectors)
+
+    first, second = near_steps(list_ref, HALO, targets, tables, near, highs, lows)
+    pipelined(list_ref[COUNTS + 1], GROUP, first, second)
+    pipelined(list_ref[COUNTS + 2], GROUP, far_first, far_second)
+
+    for copy in late_in:
+        copy.wait()
     local[30] += dot3(jnp.where(low_mask, local[31] + top, 0.0)[:, :RANK], transfer[30])
     for p in range(30, 15, -1):
         q = 2 * p - LEAVES
         both = dot3(spread_pair(local[p]), transfer[q : q + 2].reshape(128, 128))
         local[q] += both[:vectors]
         local[q + 1] += both[vectors:]
-    matrices_in[1].wait()
     out = []
     for p in range(LEAVES // 2):
         both = dot3(spread_pair(local[p]), basis[2 * p : 2 * p + 2].reshape(128, PTS))
         for c in range(2):
             lanes = slice((2 * p + c) * PTS, (2 * p + c + 1) * PTS)
-            near[:, lanes] = both[c * vectors : (c + 1) * vectors] + NEAR_WEIGHT * near[:, lanes]
+            close = near[:, lanes] + near_local[:, lanes]
+            near[:, lanes] = both[c * vectors : (c + 1) * vectors] + NEAR_WEIGHT * close
         if p % 4 == 3:
             lanes = slice((p - 3) * 2 * PTS, (p + 1) * 2 * PTS)
             out.append(start(near.at[:, lanes], out_hbm.at[:, lanes]))
@@ -510,58 +572,84 @@
     height = 2 * vectors + ROWS
     shape = jax.ShapeDtypeStruct
     select, select_t = selections()
-    params = pltpu.CompilerParams(vmem_limit_bytes=56 << 20)
+    params = pltpu.CompilerParams(vmem_limit_bytes=(64 << 20) - (64 << 10))
     smem = pltpu.SMEM
     vmem = pltpu.VMEM
     matrices = [vmem((LEAVES, RANK, PTS), F32), vmem((LEAVES - 1, RANK, 128), F32)]
-    up, down, root, local_list, halo_list, steps, counts, entries = pl.pallas_call(
+    list_shape = (LISTS,)
+    up, down, root, lists, entries = pl.pallas_call(
         up_kernel,
         out_shape=[
             shape((height, HALF), F32),
             shape((height, HALF), F32),
             shape((groups, vectors, 128), F32),
-            shape((LEAVES * SLOTS + PAD,), jnp.int32),
-            shape((LEAVES * SLOTS + PAD,), jnp.int32),
-            shape((2 * QUADS + PAD,), jnp.int32),
-            shape((3,), jnp.int32),
+            shape(list_shape, jnp.int32),
             shape((SLOTS, 64), jnp.int32),
         ],
-        in_specs=whole(2, smem) + whole(1) + whole(1, pl.ANY) + whole(1) + whole(2, pl.ANY),
-        out_specs=whole(2, pl.ANY) + whole(1) + whole(4, smem) + whole(1),
-        scratch_shapes=[vmem((vectors, points), F32), vmem((ROWS, points), F32)]
+        in_specs=whole(6, pl.ANY),
+        out_specs=whole(5, pl.ANY),
+        scratch_shapes=[
+            smem((SLOTS, LEAVES), jnp.int32),
+            smem((SLOTS, NODES), jnp.int32),
+            vmem((SLOTS, NODES), jnp.int32),
+            vmem((3, points), F32),
+            vmem((groups, vectors, 128), F32),
+            smem(list_shape, jnp.int32),
+            vmem((SLOTS, 64), jnp.int32),
+            vmem((vectors, points), F32),
+            vmem((ROWS, points), F32),
+        ]
         + matrices
-        + [vmem((vectors, 32 * 128), F32), pltpu.SemaphoreType.DMA((20,))],
+        + [vmem((vectors, 32 * 128), F32), pltpu.SemaphoreType.DMA((24,))],
         compiler_params=params,
-    )(near_lists.T, far_lists.T, far_lists.T, charges, coordinates, leaf_basis, local_transfer)
+    )(near_lists.T, far_lists.T, charges, coordinates, leaf_basis, local_transfer)
 
     upward = [(i, i + 1) for i in range(groups - 1)]
     lower = lax.ppermute(up, AXES, upward)
     upper = lax.ppermute(down, AXES, [(j, i) for i, j in upward])
     roots = lax.all_to_all(root, AXES, 0, 0)
 
-    tiles = [vmem((PTS, PTS), BF16)] * (4 * GROUP)
-    tables = [vmem((LEAVES + 1, PTS, 32), BF16), vmem((LEAVES + 1, 2 * vectors, PTS), BF16)]
+    tile = vmem((PTS, PTS), BF16)
+    tables = [
+        vmem((LEAVES + 1, PTS, 32), BF16),
+        vmem((LEAVES + 1, 2 * vectors, PTS), BF16),
+    ]
+    selects = [vmem(select.shape, BF16), vmem(select_t.shape, BF16)]
     near, targets = pl.pallas_call(
         near_kernel,
         out_shape=[shape((vectors, points), F32), shape((LEAVES, 32, PTS), BF16)],
-        in_specs=whole(2, smem) + whole(1, pl.ANY) + whole(3),
-        out_specs=whole(1) + whole(1, pl.ANY),
-        scratch_shapes=[vmem((vectors, points), F32), vmem((LEAVES, 32, PTS), BF16)]
+        in_specs=whole(5, pl.ANY),
+        out_specs=whole(2, pl.ANY),
+        scratch_shapes=[smem(list_shape, jnp.int32), vmem((3, points), F32)]
+        + selects
+        + [vmem((vectors, points), F32)] * 2
+        + [vmem((LEAVES, 32, PTS), BF16)]
         + tables
-        + [pltpu.SemaphoreType.DMA((5,))]
-        + tiles,
+        + [pltpu.SemaphoreType.DMA((10,))]
+        + [tile] * (4 * LOCAL_GROUP),
         compiler_params=params,
         cost_estimate=pl.CostEstimate(
             flops=192 * 3 * 2 * PTS**3, transcendentals=192 * PTS**2, bytes_accessed=4 << 20
         ),
-    )(counts, local_list, charges, coordinates, select, select_t)
-
+    )(lists, charges, coordinates, select, select_t)
+
+    skeletons = skeleton.transpose(1, 2, 0)
     return pl.pallas_call(
         functools.partial(down_kernel, groups),
         out_shape=shape((vectors, points), F32),
-        in_specs=whole(4, smem) + whole(7, pl.ANY) + whole(6),
+        in_specs=whole(15, pl.ANY),
         out_specs=pl.BlockSpec(memory_space=pl.ANY),
-        scratch_shapes=[vmem((vectors, points), F32), vmem((LEAVES, 32, PTS), BF16)]
+        scratch_shapes=[
+            smem(list_shape, jnp.int32),
+            smem((SLOTS, 64), jnp.int32),
+            vmem((groups, vectors, 128), F32),
+            vmem(skeletons.shape, F32),
+            vmem(top_transfer.shape, F32),
+            vmem(top_skeleton.shape, F32),
+        ]
+        + selects
+        + [vmem((vectors, points), F32)] * 2
+        + [vmem((LEAVES, 32, PTS), BF16)]
         + [vmem((height, HALF), F32)] * 3
         + matrices
         + tables
@@ -574,14 +662,13 @@
             vmem((EMPTY + 1, 2 * vectors, 128), BF16),
             vmem((2 * QUADS + 2, vectors, 128), F32),
             vmem((groups, vectors, 128), F32),
-            pltpu.SemaphoreType.DMA((16,)),
+            pltpu.SemaphoreType.DMA((24,)),
         ]
-        + tiles,
+        + [tile] * (4 * GROUP),
         compiler_params=params,
     )(
-        counts, halo_list, steps, entries, near, targets, lower, up, upper,
-        leaf_basis, local_transfer, roots, skeleton.transpose(1, 2, 0),
-        top_transfer, top_skeleton, select, select_t,
+        lists, entries, near, targets, lower, up, upper, leaf_basis, local_transfer,
+        roots, skeletons, top_transfer, top_skeleton, select, select_t,
     )
 
 

time: 58.4 us -> 53.6 us (0.918)
  Pallas kernels: 45 us -> 41.6 us
  local copies, waits for them, and re-layouts: 1.42 us -> 0 us
    pallas_call x1, Pallas kernels: 19.6 us -> 17.8 us  [on_device(): pl.pallas_call(near_kernel, out_shape=[shape((vectors, points), F32), sha...]
    unnamed x6 -> x0, local copies, waits for them, and re-layouts: 1.42 us -> none
    pallas_call x1, Pallas kernels: 18 us -> 17.2 us  [on_device(): pl.pallas_call(functools.partial(down_kernel, groups), out_shape=shape((v...]
    pallas_call x1, Pallas kernels: 7.41 us -> 6.66 us  [on_device(): pl.pallas_call(up_kernel, out_shape=[shape((height, HALF), F32), shape((h...]
where the time goes in v3:
time: 53.6 us
  Pallas kernels  41.6 us (78%)
  starting transfers between devices  11.9 us (22%)
    pallas_call x1, Pallas kernels, on_device(): pl.pallas_call(near_kernel, out_shape=[shape((vectors, points), F32), sha...  17.8 us
    pallas_call x1, Pallas kernels, on_device(): pl.pallas_call(functools.partial(down_kernel, groups), out_shape=shape((v...  17.2 us
    pallas_call x1, Pallas kernels, on_device(): pl.pallas_call(up_kernel, out_shape=[shape((height, HALF), F32), shape((h...  6.66 us
    all_to_all x1, starting transfers between devices, on_device(): roots = lax.all_to_all(root, AXES, 0, 0)  6.39 us
    ppermute x1, starting transfers between devices, on_device(): lower = lax.ppermute(up, AXES, upward)  3.64 us
    ppermute x1, starting transfers between devices, on_device(): upper = lax.ppermute(down, AXES, [(j, i) for i, j in upward])  1.91 us
  transfers between devices with their start and end apart: 3, of which 0 were waited for; matrix products, arithmetic and copies ran while one was open for 0% of the time, Pallas kernels for 33%

profile of v3, /device:TPU:1, one launch (start us, length us, event | category | flops | bytes accessed | tf_op | source)
XLA Modules:
  0.0 53.6 jit_solution(1599453615061933043)
XLA Ops:
  0.0 6.7 %shard_map.109 = (f32[72,4096]{1,0:T(8,128)}, f32[72,4096]{1,0:T(8,128)}, f32[8,32,128]{2,1,0:T(8,128)}, s32[608]{0:T(1024)}, s32[8,64]{1,0:T(8,128)}) custom-call(s32[8,32]{1,0:T(8,128)} %bitcast.4, s32[8,63]{1,0:T(8,128)} %bitcast.5, f32[32,8192]{1,0:T(8,128)} %charges_hbm.3, f32[3,8192]{1,0:T(4,128)} %coords_hbm.3, f32[32,64,256]{2,1,0:T(8,128)} %basis_hbm.3, ...), custom_call_target="tpu_custom_call" | custom-call | tf_op jit(solution)/shard_map/pallas_call | solution.py:580
  6.7 6.4 %all-to-all-start = ((f32[8,32,128]{2,1,0:T(8,128)}), f32[8,32,128]{2,1,0:T(8,128)}, u32[]{:S(2)}, u32[]{:S(2)}) async-start(f32[8,32,128]{2,1,0:T(8,128)} %get-tuple-element.18), calls=%async_computation | async-start | bytes 262144 | tf_op jit(solution)/shard_map/all_to_all | solution.py:610
  13.1 1.9 %collective-permute-start.1 = (f32[72,4096]{1,0:T(8,128)}, f32[72,4096]{1,0:T(8,128)}, u32[]{:S(2)}, u32[]{:S(2)}) collective-permute-start(f32[72,4096]{1,0:T(8,128)} %get-tuple-element.17), channel_id=1, source_target_pairs={{1,0},{4,1},{5,4},{8,5},{9,8},{12,9},{13,12},{3,2},{6,3},{7,6},{10... | collective-permute-start | bytes 3538952 | tf_op jit(solution)/shard_map/ppermute | solution.py:609
  15.0 3.6 %collective-permute-start = (f32[72,4096]{1,0:T(8,128)}, f32[72,4096]{1,0:T(8,128)}, u32[]{:S(2)}, u32[]{:S(2)}) collective-permute-start(f32[72,4096]{1,0:T(8,128)} %get-tuple-element.16.own_hbm), channel_id=1, source_target_pairs={{0,1},{1,4},{4,5},{5,8},{8,9},{9,12},{12,13},{2,3},{3,6},{6,7},{7,... | collective-permute-start | bytes 3538952 | tf_op jit(solution)/shard_map/ppermute | solution.py:608
  18.6 17.8 %shard_map.110 = (f32[32,8192]{1,0:T(8,128)}, bf16[32,32,256]{2,1,0:T(8,128)(2,1)}) custom-call(s32[608]{0:T(1024)} %get-tuple-element.12.list_hbm, f32[32,8192]{1,0:T(8,128)} %charges_hbm.3, f32[3,8192]{1,0:T(4,128)} %coords_hbm.3, bf16[64,128]{1,0:T(8,128)(2,1)} %constant.4.clone.select_hbm, bf16[32,64]{1,0:T(8,128)(2,1)} %constant.5.clone.select_t_hbm), custom_call_target="tpu_custom_call" | custom-call | flops 19327352832 | bytes 4194304 | tf_op jit(solution)/shard_map/pallas_call | solution.py:618
  36.4 0.0 all-to-all-done.roots_hbm
  36.4 0.0 collective-permute-done.1.upper_hbm
  36.4 0.0 collective-permute-done.lower_hbm
  36.4 17.2 %shard_map.111 = f32[32,8192]{1,0:T(8,128)} custom-call(s32[608]{0:T(1024)} %get-tuple-element.12.list_hbm, s32[8,64]{1,0:T(8,128)} %get-tuple-element.13.entry_hbm, f32[32,8192]{1,0:T(8,128)} %get-tuple-element.14.near_hbm, bf16[32,32,256]{2,1,0:T(8,128)(2,1)} %get-tuple-element.15.targets_hbm, f32[72,4096]{1,0:T(8,128)} %collective-permute-done.lower_hbm, ...), custom_call_target="tpu_custom_call" | custom-call | tf_op jit(solution)/shard_map/pallas_call | solution.py:637
Async XLA Ops:
  6.7 29.7 %all-to-all-start = ((f32[8,32,128]{2,1,0:T(8,128)}), f32[8,32,128]{2,1,0:T(8,128)}, u32[]{:S(2)}, u32[]{:S(2)}) async-start(f32[8,32,128]{2,1,0:T(8,128)} %get-tuple-element.18), calls=%async_computation | async-start | bytes 262144 | tf_op jit(solution)/shard_map/all_to_all | solution.py:610
  13.1 23.3 %collective-permute-start.1 = (f32[72,4096]{1,0:T(8,128)}, f32[72,4096]{1,0:T(8,128)}, u32[]{:S(2)}, u32[]{:S(2)}) collective-permute-start(f32[72,4096]{1,0:T(8,128)} %get-tuple-element.17), channel_id=1, source_target_pairs={{1,0},{4,1},{5,4},{8,5},{9,8},{12,9},{13,12},{3,2},{6,3},{7,6},{10... | collective-permute-start | bytes 3538952 | tf_op jit(solution)/shard_map/ppermute | solution.py:609
  15.0 21.4 %collective-permute-start = (f32[72,4096]{1,0:T(8,128)}, f32[72,4096]{1,0:T(8,128)}, u32[]{:S(2)}, u32[]{:S(2)}) collective-permute-start(f32[72,4096]{1,0:T(8,128)} %get-tuple-element.16.own_hbm), channel_id=1, source_target_pairs={{0,1},{1,4},{4,5},{5,8},{8,9},{9,12},{12,13},{2,3},{3,6},{6,7},{7,... | collective-permute-start | bytes 3538952 | tf_op jit(solution)/shard_map/ppermute | solution.py:608

commit v4 on v3

--- a/solution.py
+++ b/solution.py
@@ -114,37 +114,41 @@
     return jnp.concatenate([jnp.where(low, pair, zero), jnp.where(low, zero, pair)], axis=0)
 
 
-def pipelined(steps, group, first, second):
+def pipelined(begin, end, group, stages):
+    def first(base, h):
+        for u in range(group):
+            for stage in stages:
+                stage[0](base + u, u, h)
+
+    def second(base, h):
+        for u in range(group):
+            for stage in stages:
+                stage[1](base + u, u, h)
+
     def both(base, h):
-        for u in range(group):
-            first(base + group + u, u, 1 - h)
-        for u in range(group):
-            second(base + u, u, h)
-
-    def last(base, h):
-        for u in range(group):
-            second(base + u, u, h)
-
-    for u in range(group):
-        first(u, u, 0)
-    more = jnp.maximum((steps + group - 1) // group, 1) - 1
+        first(base + group, 1 - h)
+        second(base, h)
+
+    first(begin, 0)
+    more = (end - begin) // group - 1
 
     def body(i, carry):
-        both(2 * i * group, 0)
-        both((2 * i + 1) * group, 1)
+        base = begin + 2 * i * group
+        both(base, 0)
+        both(base + group, 1)
         return carry
 
     lax.fori_loop(0, more // 2, body, 0)
-    base = more // 2 * 2 * group
+    base = begin + more // 2 * 2 * group
 
     @pl.when(more % 2 == 1)
     def _():
         both(base, 0)
-        last(base + group, 1)
+        second(base + group, 1)
 
     @pl.when(more % 2 == 0)
     def _():
-        last(base, 0)
+        second(base, 0)
 
 
 class Copies:
@@ -160,16 +164,15 @@
 
 
 def up_kernel(
-    near_hbm, far_hbm, charges_hbm, coords_hbm, basis_hbm, transfer_hbm,
-    up_hbm, down_hbm, root_hbm, list_hbm, entry_hbm,
-    near_ref, far_ref, far_vec, coords, root_ref, list_ref, entry_ref,
+    charges_hbm, coords_hbm, basis_hbm, transfer_hbm,
+    up_hbm, down_hbm, root_hbm,
+    coords, root_ref,
     charges, points, basis, transfer, coef, sems,
 ):
     vectors = charges.shape[0]
     start = Copies(sems).start
     quarter = LEAVES // 4
-    in_lists = [start(near_hbm, near_ref), start(far_hbm, far_ref)]
-    in_vectors = [start(far_hbm, far_vec), start(coords_hbm, coords)]
+    in_coords = start(coords_hbm, coords)
     incoming = []
 
     def fetch(i):
@@ -181,56 +184,11 @@
     for i in range(4):
         fetch(i)
     in_transfer = start(transfer_hbm, transfer)
-    device = lax.axis_index(AXES)
-    first = device * LEAVES
-    for copy in in_lists:
-        copy.wait()
-
-    def scan_leaf(t, counts):
-        here, there = counts
-        for e in range(SLOTS):
-            entry = near_ref[e, t]
-            s = entry - first
-            inside = jnp.logical_and(s >= 0, s < LEAVES)
-            outside = jnp.logical_and(entry >= 0, jnp.logical_not(inside))
-            list_ref[here] = t * 256 + s
-            list_ref[there] = t * 256 + jnp.where(s < 0, s + REACH, s - REACH)
-            here = here + inside.astype(jnp.int32)
-            there = there + outside.astype(jnp.int32)
-        return here, there
-
-    here, there = lax.fori_loop(0, LEAVES, scan_leaf, (jnp.int32(0), jnp.int32(HALO)))
-    for u in range(PAD):
-        list_ref[here + u] = LEAVES
-        list_ref[there + u] = LEAVES
-    for q in range(QUADS):
-        list_ref[STEPS + q] = q * 256 + 2 * q
-
-    def scan_quad(q, count):
-        top = far_ref[4, 4 * q]
-        for e in range(4):
-            for c in range(4):
-                top = jnp.maximum(top, far_ref[4 + e, jnp.minimum(4 * q + c, NODES - 1)])
-        list_ref[count] = q * 256 + 2 * q + 1
-        return count + (top >= 0).astype(jnp.int32)
-
-    total = lax.fori_loop(0, QUADS, scan_quad, jnp.int32(STEPS + QUADS))
-    for u in range(PAD):
-        list_ref[total + u] = QUADS * 256
-    list_ref[COUNTS] = here
-    list_ref[COUNTS + 1] = there - HALO
-    list_ref[COUNTS + 2] = total - STEPS
-    for copy in in_vectors:
-        copy.wait()
-    entry = far_vec[...]
-    entry_ref[:, 0:NODES] = jnp.where(entry >= 0, entry - (device - 1) * NODES, EMPTY)
-    entry_ref[:, NODES:64] = jnp.full((SLOTS, 1), EMPTY, jnp.int32)
+    in_coords.wait()
     points[0:3] = coords[...]
     points[3:] = jnp.zeros((ROWS - 3, points.shape[1]), F32)
 
     out = [
-        start(list_ref, list_hbm),
-        start(entry_ref, entry_hbm),
         start(points.at[:, HALF:], up_hbm.at[2 * vectors :]),
         start(points.at[:, :HALF], down_hbm.at[2 * vectors :]),
     ]
@@ -308,9 +266,9 @@
 
 
 def near_kernel(
-    list_hbm, charges_hbm, coords_hbm, select_hbm, select_t_hbm,
-    near_hbm, targets_hbm,
-    list_ref, coords, select, select_t, near_ref,
+    near_lists_hbm, far_hbm, charges_hbm, coords_hbm, select_hbm, select_t_hbm,
+    near_hbm, targets_hbm, list_hbm, entry_hbm,
+    near_lists, far_ref, far_vec, list_ref, entry_ref, coords, select, select_t, near_ref,
     charges, targets, *rest,
 ):
     tables, sems, tiles = rest[:2], rest[2], rest[3:]
@@ -318,13 +276,27 @@
     lows = (tiles[2 * LOCAL_GROUP : 3 * LOCAL_GROUP], tiles[3 * LOCAL_GROUP :])
     start = Copies(sems).start
     quarter = LEAVES // 4
+    in_lists = [
+        start(near_lists_hbm, near_lists),
+        start(far_hbm, far_ref),
+        start(far_hbm, far_vec),
+    ]
     small = [start(coords_hbm, coords), start(select_hbm, select), start(select_t_hbm, select_t)]
     copies = []
     for i in range(4):
         lanes = slice(i * quarter * PTS, (i + 1) * quarter * PTS)
         copies.append(start(charges_hbm.at[:, lanes], charges.at[:, lanes]))
-    in_list = start(list_hbm, list_ref)
     near_ref[...] = jnp.zeros_like(near_ref)
+    device = lax.axis_index(AXES)
+    first = device * LEAVES
+    for copy in in_lists:
+        copy.wait()
+    for q in range(QUADS):
+        list_ref[STEPS + q] = q * 256 + 2 * q
+    here, there, total = jnp.int32(0), jnp.int32(HALO), jnp.int32(STEPS + QUADS)
+    entry = far_vec[...]
+    entry_ref[:, 0:NODES] = jnp.where(entry >= 0, entry - (device - 1) * NODES, EMPTY)
+    entry_ref[:, NODES:64] = jnp.full((SLOTS, 1), EMPTY, jnp.int32)
     for copy in small:
         copy.wait()
     for k in range(LEAVES):
@@ -334,14 +306,39 @@
         c = padded(scaled(coords[:, lanes]))
         parts = source_tables(k, charges[:, lanes], c, select, *tables)
         targets[k] = dot(select_t[...], parts).astype(BF16)
+        for e in range(SLOTS):
+            entry = near_lists[e, k]
+            s = entry - first
+            inside = jnp.logical_and(s >= 0, s < LEAVES)
+            outside = jnp.logical_and(entry >= 0, jnp.logical_not(inside))
+            list_ref[here] = k * 256 + s
+            list_ref[there] = k * 256 + jnp.where(s < 0, s + REACH, s - REACH)
+            here = here + inside.astype(jnp.int32)
+            there = there + outside.astype(jnp.int32)
+        if k < QUADS:
+            columns = range(4 * k, min(4 * k + 4, NODES))
+            tail = [far_ref[4 + e, c] for e in range(4) for c in columns]
+            list_ref[total] = k * 256 + 2 * k + 1
+            total = total + (functools.reduce(jnp.maximum, tail) >= 0).astype(jnp.int32)
+    for u in range(PAD):
+        list_ref[here + u] = LEAVES
+        list_ref[there + u] = LEAVES
+        list_ref[total + u] = QUADS * 256
+    list_ref[COUNTS] = here
+    list_ref[COUNTS + 1] = there - HALO
+    list_ref[COUNTS + 2] = total - STEPS
     empty_source(*tables)
-    out = start(targets, targets_hbm)
-    in_list.wait()
-    first, second = near_steps(list_ref, 0, targets, tables, near_ref, highs, lows)
-    pipelined(list_ref[COUNTS], LOCAL_GROUP, first, second)
-    out_near = start(near_ref, near_hbm)
-    out.wait()
-    out_near.wait()
+    outs = [
+        start(targets, targets_hbm),
+        start(list_ref, list_hbm),
+        start(entry_ref, entry_hbm),
+    ]
+    stage = near_steps(list_ref, 0, targets, tables, near_ref, highs, lows)
+    groups = (list_ref[COUNTS] + LOCAL_GROUP - 1) // LOCAL_GROUP
+    pipelined(0, jnp.maximum(groups, 1) * LOCAL_GROUP, LOCAL_GROUP, [stage])
+    outs.append(start(near_ref, near_hbm))
+    for copy in outs:
+        copy.wait()
 
 
 def down_kernel(
@@ -357,7 +354,9 @@
 ):
     tables = (sources, weights)
     highs = (tiles[:GROUP], tiles[GROUP : 2 * GROUP])
-    lows = (tiles[2 * GROUP : 3 * GROUP], tiles[3 * GROUP :])
+    lows = (tiles[2 * GROUP : 3 * GROUP], tiles[3 * GROUP : 4 * GROUP])
+    far_highs = (tiles[4 * GROUP : 5 * GROUP], tiles[5 * GROUP : 6 * GROUP])
+    far_lows = (tiles[6 * GROUP : 7 * GROUP], tiles[7 * GROUP :])
     vectors = near.shape[0]
     device = lax.axis_index(AXES)
     low_mask = lower_lanes(vectors)
@@ -515,8 +514,8 @@
                 value = jnp.where(lane_group == i, feature[picks[i][e]], value)
             rows.append(value)
         high, low = halves(lax.rsqrt(dot(jnp.concatenate(rows, axis=0), quads[q])))
-        highs[b][u][...] = high
-        lows[b][u][...] = low
+        far_highs[b][u][...] = high
+        far_lows[b][u][...] = low
 
     def far_second(j, u, b):
         target, q, picks = entries(j)
@@ -525,16 +524,34 @@
             left = coef_low[s[0]] + coef_high[s[1]]
             right = coef_low[s[2]] + coef_high[s[3]]
             sides.append(jnp.concatenate([left, right], axis=1))
-        high = jnp.concatenate([side[:vectors] for side in sides], axis=0)
-        low = jnp.concatenate([side[vectors:] for side in sides], axis=0)
-        both = dot(jnp.concatenate([high, low], axis=0), highs[b][u][...])
-        value = both[: 4 * vectors] + both[4 * vectors :] + dot(high, lows[b][u][...])
-        local[2 * target] += diagonal(value[: 2 * vectors, :128], vectors)
-        local[2 * target + 1] += diagonal(value[2 * vectors :, 128:], vectors)
-
-    first, second = near_steps(list_ref, HALO, targets, tables, near, highs, lows)
-    pipelined(list_ref[COUNTS + 1], GROUP, first, second)
-    pipelined(list_ref[COUNTS + 2], GROUP, far_first, far_second)
+        for p in range(2):
+            pair = sides[2 * p : 2 * p + 2]
+            high = [side[:vectors] for side in pair]
+            low = [side[vectors:] for side in pair]
+            lanes = slice(p * 128, (p + 1) * 128)
+            both = dot(jnp.concatenate(high + low, axis=0), far_highs[b][u][:, lanes])
+            rest = dot(jnp.concatenate(high, axis=0), far_lows[b][u][:, lanes])
+            value = both[: 2 * vectors] + both[2 * vectors :] + rest
+            local[2 * target + p] += diagonal(value, vectors)
+
+    near_stage = near_steps(list_ref, HALO, targets, tables, near, highs, lows)
+    far_stage = (far_first, far_second)
+    near_end = (list_ref[COUNTS + 1] + GROUP - 1) // GROUP * GROUP
+    far_end = (list_ref[COUNTS + 2] + GROUP - 1) // GROUP * GROUP
+    shared = jnp.minimum(near_end, far_end)
+
+    @pl.when(shared > 0)
+    def _():
+        pipelined(0, shared, GROUP, [near_stage, far_stage])
+
+    @pl.when(near_end > shared)
+    def _():
+        pipelined(shared, near_end, GROUP, [near_stage])
+
+    @pl.when(far_end > shared)
+    def _():
+        pipelined(shared, far_end, GROUP, [far_stage])
+
 
     for copy in late_in:
         copy.wait()
@@ -577,32 +594,25 @@
     vmem = pltpu.VMEM
     matrices = [vmem((LEAVES, RANK, PTS), F32), vmem((LEAVES - 1, RANK, 128), F32)]
     list_shape = (LISTS,)
-    up, down, root, lists, entries = pl.pallas_call(
+    up, down, root = pl.pallas_call(
         up_kernel,
         out_shape=[
             shape((height, HALF), F32),
             shape((height, HALF), F32),
             shape((groups, vectors, 128), F32),
-            shape(list_shape, jnp.int32),
-            shape((SLOTS, 64), jnp.int32),
         ],
-        in_specs=whole(6, pl.ANY),
-        out_specs=whole(5, pl.ANY),
+        in_specs=whole(4, pl.ANY),
+        out_specs=whole(3, pl.ANY),
         scratch_shapes=[
-            smem((SLOTS, LEAVES), jnp.int32),
-            smem((SLOTS, NODES), jnp.int32),
-            vmem((SLOTS, NODES), jnp.int32),
             vmem((3, points), F32),
             vmem((groups, vectors, 128), F32),
-            smem(list_shape, jnp.int32),
-            vmem((SLOTS, 64), jnp.int32),
             vmem((vectors, points), F32),
             vmem((ROWS, points), F32),
         ]
         + matrices
         + [vmem((vectors, 32 * 128), F32), pltpu.SemaphoreType.DMA((24,))],
         compiler_params=params,
-    )(near_lists.T, far_lists.T, charges, coordinates, leaf_basis, local_transfer)
+    )(charges, coordinates, leaf_basis, local_transfer)
 
     upward = [(i, i + 1) for i in range(groups - 1)]
     lower = lax.ppermute(up, AXES, upward)
@@ -615,23 +625,35 @@
         vmem((LEAVES + 1, 2 * vectors, PTS), BF16),
     ]
     selects = [vmem(select.shape, BF16), vmem(select_t.shape, BF16)]
-    near, targets = pl.pallas_call(
+    near, targets, lists, entries = pl.pallas_call(
         near_kernel,
-        out_shape=[shape((vectors, points), F32), shape((LEAVES, 32, PTS), BF16)],
-        in_specs=whole(5, pl.ANY),
-        out_specs=whole(2, pl.ANY),
-        scratch_shapes=[smem(list_shape, jnp.int32), vmem((3, points), F32)]
+        out_shape=[
+            shape((vectors, points), F32),
+            shape((LEAVES, 32, PTS), BF16),
+            shape(list_shape, jnp.int32),
+            shape((SLOTS, 64), jnp.int32),
+        ],
+        in_specs=whole(6, pl.ANY),
+        out_specs=whole(4, pl.ANY),
+        scratch_shapes=[
+            smem((SLOTS, LEAVES), jnp.int32),
+            smem((SLOTS, NODES), jnp.int32),
+            vmem((SLOTS, NODES), jnp.int32),
+            smem(list_shape, jnp.int32),
+            vmem((SLOTS, 64), jnp.int32),
+            vmem((3, points), F32),
+        ]
         + selects
         + [vmem((vectors, points), F32)] * 2
         + [vmem((LEAVES, 32, PTS), BF16)]
         + tables
-        + [pltpu.SemaphoreType.DMA((10,))]
+        + [pltpu.SemaphoreType.DMA((16,))]
         + [tile] * (4 * LOCAL_GROUP),
         compiler_params=params,
         cost_estimate=pl.CostEstimate(
             flops=192 * 3 * 2 * PTS**3, transcendentals=192 * PTS**2, bytes_accessed=4 << 20
         ),
-    )(lists, charges, coordinates, select, select_t)
+    )(near_lists.T, far_lists.T, charges, coordinates, select, select_t)
 
     skeletons = skeleton.transpose(1, 2, 0)
     return pl.pallas_call(
@@ -664,7 +686,7 @@
             vmem((groups, vectors, 128), F32),
             pltpu.SemaphoreType.DMA((24,)),
         ]
-        + [tile] * (4 * GROUP),
+        + [tile] * (8 * GROUP),
         compiler_params=params,
     )(
         lists, entries, near, targets, lower, up, upper, leaf_basis, local_transfer,

time: 53.6 us -> 51.5 us (0.961); the launches traced: 53.6 us -> 50.8 us
  Pallas kernels: 41.6 us -> 38.6 us
    pallas_call x1, Pallas kernels: 6.66 us -> 4.48 us  [on_device(): pl.pallas_call(up_kernel, out_shape=[shape((height, HALF), F32), shape((h...]
    pallas_call x1, Pallas kernels: 17.8 us -> 16.4 us  [on_device(): pl.pallas_call(near_kernel, out_shape=[shape((vectors, points), F32), sha...]
  transfers between devices with their start and end apart: 3 -> 3, of which waited for: 0 -> 0; matrix products, arithmetic and copies ran while one was open for 0% -> 0% of each run, Pallas kernels for 33% -> 32%
where the time goes in v4:
time: 51.5 us; the launch traced here: 50.8 us
  Pallas kernels  38.6 us (75%)
  starting transfers between devices  11.9 us (23%)
    pallas_call x1, Pallas kernels, on_device(): pl.pallas_call(functools.partial(down_kernel, groups), out_shape=shape((v...  17.7 us
    pallas_call x1, Pallas kernels, on_device(): pl.pallas_call(near_kernel, out_shape=[shape((vectors, points), F32), sha...  16.4 us
    all_to_all x1, starting transfers between devices, on_device(): roots = lax.all_to_all(root, AXES, 0, 0)  6.39 us
    pallas_call x1, Pallas kernels, on_device(): pl.pallas_call(up_kernel, out_shape=[shape((height, HALF), F32), shape((h...  4.48 us
    ppermute x1, starting transfers between devices, on_device(): lower = lax.ppermute(up, AXES, upward)  3.64 us
    ppermute x1, starting transfers between devices, on_device(): upper = lax.ppermute(down, AXES, [(j, i) for i, j in upward])  1.91 us
  transfers between devices with their start and end apart: 3, of which 0 were waited for; matrix products, arithmetic and copies ran while one was open for 0% of the time, Pallas kernels for 32%

profile of v4, /device:TPU:1, one launch (start us, length us, event | category | flops | bytes accessed | tf_op | source)
XLA Modules:
  0.0 50.8 jit_solution(11685056959979507731)
XLA Ops:
  0.0 4.5 %shard_map.110 = (f32[72,4096]{1,0:T(8,128)}, f32[72,4096]{1,0:T(8,128)}, f32[8,32,128]{2,1,0:T(8,128)}) custom-call(f32[32,8192]{1,0:T(8,128)} %charges_hbm.3, f32[3,8192]{1,0:T(4,128)} %coords_hbm.3, f32[32,64,256]{2,1,0:T(8,128)} %basis_hbm.3, f32[31,64,128]{2,1,0:T(8,128)} %transfer_hbm.3), custom_call_target="tpu_custom_call" | custom-call | tf_op jit(solution)/shard_map/pallas_call | solution.py:597
  4.5 6.4 %all-to-all-start = ((f32[8,32,128]{2,1,0:T(8,128)}), f32[8,32,128]{2,1,0:T(8,128)}, u32[]{:S(2)}, u32[]{:S(2)}) async-start(f32[8,32,128]{2,1,0:T(8,128)} %get-tuple-element.18), calls=%async_computation | async-start | bytes 262144 | tf_op jit(solution)/shard_map/all_to_all | solution.py:620
  10.9 1.9 %collective-permute-start.1 = (f32[72,4096]{1,0:T(8,128)}, f32[72,4096]{1,0:T(8,128)}, u32[]{:S(2)}, u32[]{:S(2)}) collective-permute-start(f32[72,4096]{1,0:T(8,128)} %get-tuple-element.17), channel_id=1, source_target_pairs={{1,0},{4,1},{5,4},{8,5},{9,8},{12,9},{13,12},{3,2},{6,3},{7,6},{10... | collective-permute-start | bytes 3538952 | tf_op jit(solution)/shard_map/ppermute | solution.py:619
  12.8 3.6 %collective-permute-start = (f32[72,4096]{1,0:T(8,128)}, f32[72,4096]{1,0:T(8,128)}, u32[]{:S(2)}, u32[]{:S(2)}) collective-permute-start(f32[72,4096]{1,0:T(8,128)} %get-tuple-element.16.own_hbm), channel_id=1, source_target_pairs={{0,1},{1,4},{4,5},{5,8},{8,9},{9,12},{12,13},{2,3},{3,6},{6,7},{7,... | collective-permute-start | bytes 3538952 | tf_op jit(solution)/shard_map/ppermute | solution.py:618
  16.5 16.4 %shard_map.109 = (f32[32,8192]{1,0:T(8,128)}, bf16[32,32,256]{2,1,0:T(8,128)(2,1)}, s32[608]{0:T(1024)}, s32[8,64]{1,0:T(8,128)}) custom-call(s32[8,32]{1,0:T(8,128)} %bitcast.4, s32[8,63]{1,0:T(8,128)} %bitcast.5, f32[32,8192]{1,0:T(8,128)} %charges_hbm.3, f32[3,8192]{1,0:T(4,128)} %coords_hbm.3, bf16[64,128]{1,0:T(8,128)(2,1)} %constant.4.clone.select_hbm, ...), custom_call_target="tpu_custom_call" | custom-call | flops 19327352832 | bytes 4194304 | tf_op jit(solution)/shard_map/pallas_call | solution.py:628
  32.9 0.0 all-to-all-done.roots_hbm
  32.9 0.0 collective-permute-done.1.upper_hbm
  32.9 0.0 collective-permute-done.lower_hbm
  32.9 17.7 %shard_map.111 = f32[32,8192]{1,0:T(8,128)} custom-call(s32[608]{0:T(1024)} %get-tuple-element.12.list_hbm, s32[8,64]{1,0:T(8,128)} %get-tuple-element.13.entry_hbm, f32[32,8192]{1,0:T(8,128)} %get-tuple-element.14.near_hbm, bf16[32,32,256]{2,1,0:T(8,128)(2,1)} %get-tuple-element.15.targets_hbm, f32[72,4096]{1,0:T(8,128)} %collective-permute-done.lower_hbm, ...), custom_call_target="tpu_custom_call" | custom-call | tf_op jit(solution)/shard_map/pallas_call | solution.py:659
Async XLA Ops:
  4.5 28.4 %all-to-all-start = ((f32[8,32,128]{2,1,0:T(8,128)}), f32[8,32,128]{2,1,0:T(8,128)}, u32[]{:S(2)}, u32[]{:S(2)}) async-start(f32[8,32,128]{2,1,0:T(8,128)} %get-tuple-element.18), calls=%async_computation | async-start | bytes 262144 | tf_op jit(solution)/shard_map/all_to_all | solution.py:620
  10.9 22.0 %collective-permute-start.1 = (f32[72,4096]{1,0:T(8,128)}, f32[72,4096]{1,0:T(8,128)}, u32[]{:S(2)}, u32[]{:S(2)}) collective-permute-start(f32[72,4096]{1,0:T(8,128)} %get-tuple-element.17), channel_id=1, source_target_pairs={{1,0},{4,1},{5,4},{8,5},{9,8},{12,9},{13,12},{3,2},{6,3},{7,6},{10... | collective-permute-start | bytes 3538952 | tf_op jit(solution)/shard_map/ppermute | solution.py:619
  12.8 20.1 %collective-permute-start = (f32[72,4096]{1,0:T(8,128)}, f32[72,4096]{1,0:T(8,128)}, u32[]{:S(2)}, u32[]{:S(2)}) collective-permute-start(f32[72,4096]{1,0:T(8,128)} %get-tuple-element.16.own_hbm), channel_id=1, source_target_pairs={{0,1},{1,4},{4,5},{5,8},{8,9},{9,12},{12,13},{2,3},{3,6},{6,7},{7,... | collective-permute-start | bytes 3538952 | tf_op jit(solution)/shard_map/ppermute | solution.py:618

commit v5 on v4

--- a/solution.py
+++ b/solution.py
@@ -677,7 +677,7 @@
         + tables
         + [
             vmem((2, 256, 128), F32),
-            vmem((128 * 8, 128), F32),
+            vmem((129 * 8, 128), F32),
             vmem((192, RANK, 128), BF16),
             vmem((QUADS, 128, 256), BF16),
             vmem((EMPTY + 1, 2 * vectors, 128), BF16),

time: 51.5 us -> 51.5 us (level)
    pallas_call x1, Pallas kernels: 16.4 us -> 17.4 us  [on_device(): pl.pallas_call(near_kernel, out_shape=[shape((vectors, points), F32), sha...]
    pallas_call x1, Pallas kernels: 17.7 us -> 16.9 us  [on_device(): pl.pallas_call(functools.partial(down_kernel, groups), out_shape=shape((v...]
  transfers between devices with their start and end apart: 3 -> 3, of which waited for: 0 -> 0; matrix products, arithmetic and copies ran while one was open for 0% -> 0% of each run, Pallas kernels for 32% -> 34%
where the time goes in v5:
time: 51.5 us; the launch traced here: 51 us
  Pallas kernels  38.8 us (75%)
  starting transfers between devices  11.9 us (23%)
    pallas_call x1, Pallas kernels, on_device(): pl.pallas_call(near_kernel, out_shape=[shape((vectors, points), F32), sha...  17.4 us
    pallas_call x1, Pallas kernels, on_device(): pl.pallas_call(functools.partial(down_kernel, groups), out_shape=shape((v...  16.9 us
    all_to_all x1, starting transfers between devices, on_device(): roots = lax.all_to_all(root, AXES, 0, 0)  6.39 us
    pallas_call x1, Pallas kernels, on_device(): pl.pallas_call(up_kernel, out_shape=[shape((height, HALF), F32), shape((h...  4.48 us
    ppermute x1, starting transfers between devices, on_device(): lower = lax.ppermute(up, AXES, upward)  3.64 us
    ppermute x1, starting transfers between devices, on_device(): upper = lax.ppermute(down, AXES, [(j, i) for i, j in upward])  1.91 us
  transfers between devices with their start and end apart: 3, of which 0 were waited for; matrix products, arithmetic and copies ran while one was open for 0% of the time, Pallas kernels for 34%

profile of v5, /device:TPU:1, one launch (start us, length us, event | category | flops | bytes accessed | tf_op | source)
XLA Modules:
  0.0 51.0 jit_solution(10977965997287163200)
XLA Ops:
  0.0 4.5 %shard_map.110 = (f32[72,4096]{1,0:T(8,128)}, f32[72,4096]{1,0:T(8,128)}, f32[8,32,128]{2,1,0:T(8,128)}) custom-call(f32[32,8192]{1,0:T(8,128)} %charges_hbm.3, f32[3,8192]{1,0:T(4,128)} %coords_hbm.3, f32[32,64,256]{2,1,0:T(8,128)} %basis_hbm.3, f32[31,64,128]{2,1,0:T(8,128)} %transfer_hbm.3), custom_call_target="tpu_custom_call" | custom-call | tf_op jit(solution)/shard_map/pallas_call | solution.py:597
  4.5 6.4 %all-to-all-start = ((f32[8,32,128]{2,1,0:T(8,128)}), f32[8,32,128]{2,1,0:T(8,128)}, u32[]{:S(2)}, u32[]{:S(2)}) async-start(f32[8,32,128]{2,1,0:T(8,128)} %get-tuple-element.18), calls=%async_computation | async-start | bytes 262144 | tf_op jit(solution)/shard_map/all_to_all | solution.py:620
  10.9 1.9 %collective-permute-start.1 = (f32[72,4096]{1,0:T(8,128)}, f32[72,4096]{1,0:T(8,128)}, u32[]{:S(2)}, u32[]{:S(2)}) collective-permute-start(f32[72,4096]{1,0:T(8,128)} %get-tuple-element.17), channel_id=1, source_target_pairs={{1,0},{4,1},{5,4},{8,5},{9,8},{12,9},{13,12},{3,2},{6,3},{7,6},{10... | collective-permute-start | bytes 3538952 | tf_op jit(solution)/shard_map/ppermute | solution.py:619
  12.8 3.6 %collective-permute-start = (f32[72,4096]{1,0:T(8,128)}, f32[72,4096]{1,0:T(8,128)}, u32[]{:S(2)}, u32[]{:S(2)}) collective-permute-start(f32[72,4096]{1,0:T(8,128)} %get-tuple-element.16.own_hbm), channel_id=1, source_target_pairs={{0,1},{1,4},{4,5},{5,8},{8,9},{9,12},{12,13},{2,3},{3,6},{6,7},{7,... | collective-permute-start | bytes 3538952 | tf_op jit(solution)/shard_map/ppermute | solution.py:618
  16.5 17.4 %shard_map.109 = (f32[32,8192]{1,0:T(8,128)}, bf16[32,32,256]{2,1,0:T(8,128)(2,1)}, s32[608]{0:T(1024)}, s32[8,64]{1,0:T(8,128)}) custom-call(s32[8,32]{1,0:T(8,128)} %bitcast.4, s32[8,63]{1,0:T(8,128)} %bitcast.5, f32[32,8192]{1,0:T(8,128)} %charges_hbm.3, f32[3,8192]{1,0:T(4,128)} %coords_hbm.3, bf16[64,128]{1,0:T(8,128)(2,1)} %constant.4.clone.select_hbm, ...), custom_call_target="tpu_custom_call" | custom-call | flops 19327352832 | bytes 4194304 | tf_op jit(solution)/shard_map/pallas_call | solution.py:628
  33.9 0.0 all-to-all-done.roots_hbm
  33.9 0.0 collective-permute-done.1.upper_hbm
  33.9 0.0 collective-permute-done.lower_hbm
  33.9 16.9 %shard_map.111 = f32[32,8192]{1,0:T(8,128)} custom-call(s32[608]{0:T(1024)} %get-tuple-element.12.list_hbm, s32[8,64]{1,0:T(8,128)} %get-tuple-element.13.entry_hbm, f32[32,8192]{1,0:T(8,128)} %get-tuple-element.14.near_hbm, bf16[32,32,256]{2,1,0:T(8,128)(2,1)} %get-tuple-element.15.targets_hbm, f32[72,4096]{1,0:T(8,128)} %collective-permute-done.lower_hbm, ...), custom_call_target="tpu_custom_call" | custom-call | tf_op jit(solution)/shard_map/pallas_call | solution.py:659
Async XLA Ops:
  4.5 29.4 %all-to-all-start = ((f32[8,32,128]{2,1,0:T(8,128)}), f32[8,32,128]{2,1,0:T(8,128)}, u32[]{:S(2)}, u32[]{:S(2)}) async-start(f32[8,32,128]{2,1,0:T(8,128)} %get-tuple-element.18), calls=%async_computation | async-start | bytes 262144 | tf_op jit(solution)/shard_map/all_to_all | solution.py:620
  10.9 23.0 %collective-permute-start.1 = (f32[72,4096]{1,0:T(8,128)}, f32[72,4096]{1,0:T(8,128)}, u32[]{:S(2)}, u32[]{:S(2)}) collective-permute-start(f32[72,4096]{1,0:T(8,128)} %get-tuple-element.17), channel_id=1, source_target_pairs={{1,0},{4,1},{5,4},{8,5},{9,8},{12,9},{13,12},{3,2},{6,3},{7,6},{10... | collective-permute-start | bytes 3538952 | tf_op jit(solution)/shard_map/ppermute | solution.py:619
  12.8 21.1 %collective-permute-start = (f32[72,4096]{1,0:T(8,128)}, f32[72,4096]{1,0:T(8,128)}, u32[]{:S(2)}, u32[]{:S(2)}) collective-permute-start(f32[72,4096]{1,0:T(8,128)} %get-tuple-element.16.own_hbm), channel_id=1, source_target_pairs={{0,1},{1,4},{4,5},{5,8},{8,9},{9,12},{12,13},{2,3},{3,6},{6,7},{7,... | collective-permute-start | bytes 3538952 | tf_op jit(solution)/shard_map/ppermute | solution.py:618
